TPU v7x, 256 devices: a whole 4x4x8 slice. The times are simulated.
256 devices in a mesh: gx: 8 (over z_lo, core), gy: 16 (over x, y), gz: 2 (over z_hi).
Axes of the slice: x: 4, y: 4, z: 8 (z_hi: 2, z_lo: 4; z = z_hi * 4 + z_lo), core: 2. Of those that a mesh axis runs over, the one named last changes fastest.
Arguments:
- displacement: float32 [3, 256, 512, 512], P(None, 'gx', 'gy', 'gz'), may hold values from -0.0018 to 0.0018
- applied_strain: float32 [6], replicated, may hold values from -0.0003 to 0.0003
- labels: int32 [256, 512, 512], P('gx', 'gy', 'gz'), may hold values from 0 to 3
- history: float32 [256, 512, 512], P('gx', 'gy', 'gz'), may hold values from 5e-05 to 0.0006
- modulus: float32 [4], replicated, may hold values from 5000 to 60000
- poisson: float32 [4], replicated, may hold values from 0.1 to 0.3
- threshold: float32 [4], replicated, may hold values from 4e-05 to 0.00016
- ductility: float32 [4], replicated, may hold values from 0.6 to 1
- brittleness: float32 [4], replicated, may hold values from 5000 to 20000
- weight: float32 [4], replicated, may hold values from 0.1 to 1
Outputs:
- damage: float32 [256, 512, 512], P('gx', 'gy', 'gz')
- mises: float32 [256, 512, 512], P('gx', 'gy', 'gz')
All inputs are finite; a program needn't handle non-finite values.
Results may differ from a plain program's by a relative error of at most 0.0003.
Values sent between devices are 32-bit elements; how exact they have to be, the bound alone decides.
No kernel may reach another device: no remote copies, remote signals or barrier semaphores. Data moves between devices by JAX's collectives and lax.ppermute only.
A program may use at most 64 MiB of HBM per device.

v0:
```python
import math

import jax
import jax.numpy as jnp
import numpy as np
from jax import lax
from jax.experimental import pallas as pl
from jax.experimental.pallas import tpu as pltpu
from jax.sharding import PartitionSpec as P


RADIUS = 8
F32 = jnp.float32
BF16 = jnp.bfloat16


def taps():
    return [math.exp(-2.0 * s * s / (RADIUS * RADIUS)) for s in range(-RADIUS, RADIUS + 1)]


def band(outs, ins, offset):
    table = taps()
    full = np.zeros((outs, ins), np.float64)
    for i in range(outs):
        for k in range(ins):
            s = k + offset - i
            if abs(s) <= RADIUS:
                full[i, k] = table[s + RADIUS]
    return full


def split_const(full):
    hi = full.astype(jnp.bfloat16)
    lo = (full - hi.astype(np.float64)).astype(jnp.bfloat16)
    return hi, lo


def split(f):
    hi = f.astype(BF16)
    lo = (f - hi.astype(F32)).astype(BF16)
    return hi, lo


def mxu(a, b, dims):
    return lax.dot_general(a, b, (dims, ((), ())), preferred_element_type=F32)


def shift_route(block, axes, steps):
    sizes = [lax.axis_size(a) for a in axes]
    total = math.prod(sizes)
    route = []
    for flat in range(total):
        place = np.unravel_index(flat, sizes)
        target = tuple((i + s) % n for i, s, n in zip(place, steps, sizes))
        route.append((flat, int(np.ravel_multi_index(target, sizes))))
    return lax.ppermute(block, axes if len(axes) > 1 else axes[0], route)


def swap_route(block, axis, parity):
    size = lax.axis_size(axis)
    route = []
    for k in range(0, size, 2):
        a, b = (k + parity) % size, (k + 1 + parity) % size
        route += [(a, b), (b, a)]
    return lax.ppermute(block, axis, route)


def call(
    kernel, outs, scratch=(), n_in=1, smem=(), limit=10 << 20, spaces=None, out_spaces=None,
    aliases=None, after=(), odd=None,
):
    spaces = (spaces or [None] * n_in) + [pl.ANY] * len(after)
    n_in = len(spaces) - len(after)

    def body(*refs):
        refs = [*refs[:n_in], *refs[n_in + len(after) :]]
        if odd is not None:
            refs.insert(odd, (lax.axis_index("gx") % 2, lax.axis_index("gy") % 2))
        kernel(*refs)

    specs = [
        pl.BlockSpec(memory_space=pltpu.SMEM if i in smem else space or pltpu.VMEM)
        for i, space in enumerate(spaces)
    ]
    built = pl.pallas_call(
        body,
        out_shape=[jax.ShapeDtypeStruct(s, F32) for s in outs],
        in_specs=specs,
        out_specs=[pl.BlockSpec(memory_space=s) for s in out_spaces or [pltpu.VMEM] * len(outs)],
        scratch_shapes=list(scratch),
        input_output_aliases=aliases or {},
        compiler_params=pltpu.CompilerParams(vmem_limit_bytes=limit),
    )
    return lambda *args: built(*args, *after)


def pick(labels, table, row):
    out = jnp.where(labels == 0, table[row, 0], table[row, 3])
    out = jnp.where(labels == 1, table[row, 1], out)
    return jnp.where(labels == 2, table[row, 2], out)


def edge_columns(field, put):
    for j in range(8):
        put(j, field(j, 0).T[0:8], field(j, 1).T[120:128])


def table_kernel(modulus, poisson, threshold, ductility, brittleness, weight, table):
    for k in range(4):
        nu, w = poisson[k], weight[k]
        lead, shear = 1.0 - 2.0 * nu, 1.0 / (1.0 + nu)
        table[0, k] = 0.45 * w / lead
        table[1, k] = 0.3 * (w * shear) * (w * shear)
        table[2, k] = w
        table[3, k] = math.sqrt(3.0) * modulus[k] * shear
        table[4, k] = threshold[k]
        table[5, k] = threshold[k] * (1.0 - ductility[k])
        table[6, k] = ductility[k]
        table[7, k] = brittleness[k]


def planes_kernel(u, xm, ym, kept, sem):
    keep = pltpu.make_async_copy(u, kept, sem.at[0])
    keep.start()
    for c in range(3):
        xm[c] = u[c, 0]
        for x in range(32):
            ym[c, x : x + 1, :] = u[c, x, 0:1, :]
    keep.wait()


def extend_kernel(ym, xm, out):
    for c in range(3):
        out[c, 0:32] = ym[c]
        out[c, 32:33, :] = xm[c, 0:1, :]


def weight_edges_kernel(weight, odd, labels, near, far, low, high, sem):
    copies = [
        pltpu.make_async_copy(labels.at[pl.ds(0, 8)], low, sem.at[0]),
        pltpu.make_async_copy(labels.at[pl.ds(24, 8)], high, sem.at[1]),
    ]
    for copy in copies:
        copy.start()
    for copy in copies:
        copy.wait()
    is_odd = odd[0] == 1

    def choose(lab):
        w = jnp.where(lab == 0, weight[0], weight[3])
        w = jnp.where(lab == 1, weight[1], w)
        return jnp.where(lab == 2, weight[2], w)

    def step(i, carry):
        a, b = choose(low[i]), choose(high[i])
        near[i] = jnp.where(is_odd, a, b)
        far[i] = jnp.where(is_odd, b, a)
        return carry

    lax.fori_loop(0, 8, step, 0, unroll=2)


def columns_kernel(u, labels, nodes):
    lane = lax.broadcasted_iota(jnp.int32, (32, 128), 1)

    def step(x, carry):
        first, last, lab = carry
        for c in range(3):
            at = 40 * c + x
            first = jnp.where(lane == at, pltpu.roll(u[c, x, :, 0:128], at, 1), first)
            last = jnp.where(lane == at, pltpu.roll(u[c, x, :, 128:256], at + 1, 1), last)
        moved = pltpu.roll(labels[x, :, 128:256], x + 1, 1)
        return first, last, jnp.where(lane == x, moved, lab)

    zero = jnp.zeros((32, 128), F32)
    first, last, lab = lax.fori_loop(
        0, 32, step, (zero, zero, jnp.zeros((32, 128), jnp.int32)), unroll=2
    )
    nodes[0:32, :] = first
    nodes[32:64, :] = last
    nodes[64:96, :] = lab.astype(F32)


def combine(d, s, dsh, ssh):
    a = [d[c] + dsh[c] for c in range(3)]
    b = [ssh[c] - s[c] for c in range(3)]
    m = [ssh[c] + s[c] for c in range(3)]
    plus = [a[0], b[1], a[1] + b[0], m[2], b[2] + m[1], a[2] + m[0]]
    minus = [a[0], b[1], a[1] + b[0], m[2], b[2] - m[1], a[2] - m[0]]
    return plus, minus


def respond(applied, table, lab, sums):
    xx = applied[0] + 0.25 * sums[0]
    yy = applied[1] + 0.25 * sums[1]
    zz = applied[2] + 0.25 * sums[2]
    xy = applied[5] + 0.125 * sums[3]
    yz = applied[3] + 0.125 * sums[4]
    xz = applied[4] + 0.125 * sums[5]
    trace = xx + yy + zz
    p, q, r = xx - yy, yy - zz, zz - xx
    second = (p * p + q * q + r * r) * (1.0 / 6.0) + (yz * yz + xz * xz + xy * xy)
    lead = pick(lab, table, 0) * trace
    value = lead + jnp.sqrt(lead * lead + pick(lab, table, 1) * second)
    return value, second


def strain_kernel(table, applied, u, xm, ym, labels, top, second):
    row = lax.broadcasted_iota(jnp.int32, (32, 256), 0)
    inside = lax.broadcasted_iota(jnp.int32, (32, 256), 1) < 255

    def cells(x, here, there, r_here, r_there):
        d, s, dsh, ssh = [], [], [], []
        for c in range(3):
            d.append(there[c] - here[c])
            s.append(there[c] + here[c])
            dsh.append(jnp.where(row == 31, r_there[c] - r_here[c], pltpu.roll(d[c], 31, 0)))
            ssh.append(jnp.where(row == 31, r_there[c] + r_here[c], pltpu.roll(s[c], 31, 0)))
        plus, minus = combine(d, s, dsh, ssh)
        shifted = [pltpu.roll(p, 255, 1) for p in plus]
        value, second[x] = respond(
            applied,
            table,
            labels[x],
            [
                minus[0] + shifted[0],
                minus[1] + shifted[1],
                shifted[3] - minus[3],
                minus[2] + shifted[2],
                minus[4] + shifted[4],
                minus[5] + shifted[5],
            ],
        )
        top[x] = jnp.where(inside, value, 0.0)

    def step(x, carry):
        cells(
            x,
            [u[c, x] for c in range(3)],
            [u[c, x + 1] for c in range(3)],
            [ym[c, pl.ds(x, 1), :] for c in range(3)],
            [ym[c, pl.ds(x + 1, 1), :] for c in range(3)],
        )
        return carry

    lax.fori_loop(0, 31, step, 0)
    cells(
        31,
        [u[c, 31] for c in range(3)],
        [xm[c] for c in range(3)],
        [ym[c, 31:32, :] for c in range(3)],
        [ym[c, 32:33, :] for c in range(3)],
    )


def columns_out(field, out, first):
    def put(j, low, high):
        at = first + 16 * j
        out[at : at + 16, :] = jnp.concatenate([high, low], axis=0)

    edge_columns(
        lambda j, t: field[4 * j : 4 * j + 4, :, 128 * t : 128 * t + 128].reshape(128, 128), put
    )


def zpack_kernel(top, nodes, xm, ym, out):
    columns_out(top, out, 0)
    lane = lax.broadcasted_iota(jnp.int32, (32, 128), 1)
    lane1 = lax.broadcasted_iota(jnp.int32, (8, 128), 1)
    pad = jnp.zeros((88, 128), F32)
    for t in range(2):
        body = nodes[32 * t : 32 * t + 32, :]
        edge = jnp.zeros((8, 128), F32)
        for c in range(3):
            at = 40 * c + 32
            lanes = slice(128 * t, 128 * t + 128)
            body = jnp.where(lane == at, pltpu.roll(xm[c, :, lanes], (at + t) % 128, 1), body)
            turned = jnp.concatenate([ym[c, :, lanes], pad], axis=0).T
            line = turned[127:128] if t else turned[0:1]
            line = pltpu.roll(jnp.broadcast_to(line, (8, 128)), 40 * c, 1)
            edge = jnp.where((lane1 >= 40 * c) & (lane1 <= at), line, edge)
        out[128 + 40 * t : 160 + 40 * t, :] = body
        out[160 + 40 * t : 168 + 40 * t, :] = edge
    out[208:240, :] = nodes[64:96, :]


def column_cells(applied, table, lower, upper, lab):
    parts = []
    for n in (lower, upper):
        nx = pltpu.roll(n, 127, 1)
        d, s = nx - n, nx + n
        dsh, ssh = pltpu.roll(d, 39, 0), pltpu.roll(s, 39, 0)
        parts.append((d + dsh, ssh - s, ssh + s))
    gx = (parts[0][0] + parts[1][0])[0:32]
    gy = (parts[0][1] + parts[1][1])[0:32]
    gz = (parts[1][2] - parts[0][2])[0:32]
    gx = [gx, pltpu.roll(gx, 88, 1), pltpu.roll(gx, 48, 1)]
    gy = [gy, pltpu.roll(gy, 88, 1), pltpu.roll(gy, 48, 1)]
    gz = [gz, pltpu.roll(gz, 88, 1), pltpu.roll(gz, 48, 1)]
    return respond(
        applied,
        table,
        lab.astype(jnp.int32),
        [gx[0], gy[1], gz[2], gx[1] + gy[0], gy[2] + gz[1], gx[2] + gz[0]],
    )


def blocks_of(cells, scratch):
    keep = lax.broadcasted_iota(jnp.int32, (32, 128), 1) < 32
    padded = jnp.concatenate([jnp.where(keep, cells, 0.0), jnp.zeros((96, 128), F32)], axis=0)
    scratch[...] = padded.T[0:32]
    total = scratch[pl.ds(0, 8, stride=4), :]
    for i in range(1, 4):
        total = total + pltpu.roll(scratch[pl.ds(i, 8, stride=4), :], 32 * i, 1)
    return total


def z_local_kernel(field, gz, out):
    for j in range(8):
        hi, lo = split(field[4 * j : 4 * j + 4].reshape(128, 256))
        part = mxu(hi, gz[0], ((1,), (0,))) + mxu(lo, gz[0], ((1,), (0,)))
        part = part + mxu(hi, gz[1], ((1,), (0,)))
        out[4 * j : 4 * j + 4] = part.reshape(4, 32, 256)


def z_halo(local, halo, gh, out, before=None, last=None):
    for j in range(8):
        lines = halo[16 * j : 16 * j + 16, :]
        if before is None:
            rows = [lines, jnp.zeros((8, 128), F32)]
        else:
            rows = [lines[0:7], before[j : j + 1], lines[8:16], last[j : j + 1], jnp.zeros((7, 128), F32)]
        chi, clo = split(jnp.concatenate(rows, axis=0).T)
        c = jnp.concatenate([chi, clo, chi], axis=1)
        part = mxu(c, gh[...], ((1,), (0,))).reshape(4, 32, 256)
        out[4 * j : 4 * j + 4] = local[4 * j : 4 * j + 4] + part


def top_z_kernel(table, applied, odd, local, mine, peer, gh, out, near, far, second_last, scratch):
    last, second_last[...] = column_cells(
        applied, table, mine[168:208, :], peer[128:168, :], mine[208:240, :]
    )
    before, _ = column_cells(applied, table, peer[168:208, :], mine[128:168, :], peer[208:240, :])
    last, before = blocks_of(last, scratch), blocks_of(before, scratch)
    z_halo(local, peer, gh, out, before, last)
    y_edges(odd, out, near, far)


def weights_z_kernel(local, peer, gh, inverse):
    z_halo(local, peer, gh, inverse)
    inverse[...] = 1.0 / inverse[...]


def y_edges(odd, out, near, far):
    start = pl.multiple_of(24 * (1 - odd[1]), 8)
    near[...] = out[:, pl.ds(start, 8), :]
    far[...] = out[:, pl.ds(pl.multiple_of(24 - start, 8), 8), :]


def smooth_x(odd, cell, r_near, r_far, out):
    is_odd = odd[0] == 1
    table = taps()

    def step(k, carry):
        rows = pl.ds(pl.multiple_of((k // 2) * 8, 8), 8)
        lanes = pl.ds(pl.multiple_of((k % 2) * 128, 128), 128)
        low, high = [], []
        for i in range(8):
            a, b = r_near[i, rows, lanes], r_far[i, rows, lanes]
            low.append(jnp.where(is_odd, a, b))
            high.append(jnp.where(is_odd, b, a))
        cells = low + [cell(i, rows, lanes) for i in range(32)] + high
        for i in range(32):
            total = table[8] * cells[i + 8]
            for s in range(1, 9):
                total = total + table[8 + s] * (cells[i + 8 - s] + cells[i + 8 + s])
            out[i, rows, lanes] = total
        return carry

    lax.fori_loop(0, 8, step, 0)


def weights_x_kernel(table, odd, labels, r_near, r_far, out, near, far):
    smooth_x(odd, lambda *at: pick(labels[at], table, 2), r_near, r_far, out)
    y_edges(odd, out, near, far)


def smooth_y(x, is_odd, field, r_near, r_far, gy):
    a, b = r_near[x], r_far[x]
    cells = jnp.concatenate([jnp.where(is_odd, a, b), field[x], jnp.where(is_odd, b, a)], axis=0)
    hi, lo = split(cells)
    return mxu(gy[...], jnp.concatenate([hi, lo, hi], axis=0), ((1,), (0,)))


def smooth_all_y(odd, field, r_near, r_far, gy, out):
    is_odd = odd[1] == 1

    def step(x, carry):
        out[x] = smooth_y(x, is_odd, field, r_near, r_far, gy)
        return carry

    lax.fori_loop(0, 32, step, 0, unroll=8)


def weights_y_kernel(odd, field, r_near, r_far, gy, gz, out, cols):
    smooth_all_y(odd, field, r_near, r_far, gy, out)
    columns_out(out, cols, 0)
    z_local_kernel(out, gz, out)


def top_y_kernel(odd, field, r_near, r_far, gy, out, near, far):
    smooth_all_y(odd, field, r_near, r_far, gy, out)
    start = 24 * (1 - odd[0])
    near[...] = out[pl.ds(start, 8)]
    far[...] = out[pl.ds(24 - start, 8)]


def stress_kernel(table, labels, second, second_last, stress):
    lane = lax.broadcasted_iota(jnp.int32, (32, 128), 1)

    def step(x, carry):
        moved = pltpu.roll(second_last[...], 127 - x, 1)
        end = jnp.where(lane == 127, moved, second[x, :, 128:256])
        whole = jnp.concatenate([second[x, :, 0:128], end], axis=1)
        stress[x] = pick(labels[x], table, 3) * jnp.sqrt(whole)
        return carry

    lax.fori_loop(0, 32, step, 0, unroll=2)


def finish_cells(table, lab, averaged, history, stress):
    kappa = jnp.maximum(history, averaged)
    start = pick(lab, table, 4)
    grown = (
        1.0
        - pick(lab, table, 5) / jnp.maximum(kappa, start)
        - pick(lab, table, 6) * jnp.exp(pick(lab, table, 7) * (start - kappa))
    )
    harm = jnp.where(kappa > start, grown, 0.0)
    return harm, (1.0 - harm) * stress


def finish_planes(
    table, window, count, first, inverse, history, stress, labels, d_buf, m_buf, damage, mises, sem
):
    g = taps()

    def step(k):
        rows = pl.ds(pl.multiple_of((k // 2) * 8, 8), 8)
        lanes = pl.ds(pl.multiple_of((k % 2) * 128, 128), 128)
        cells = [window(w, rows, lanes) for w in range(count + 16)]
        for i in range(count):
            total = g[8] * cells[i + 8]
            for s in range(1, 9):
                total = total + g[8 + s] * (cells[i + 8 - s] + cells[i + 8 + s])
            at = (first + i, rows, lanes)
            harm, von_mises = finish_cells(
                table, labels[at], total * inverse[at], history[at], stress[at]
            )
            d_buf[i, rows, lanes] = harm
            m_buf[i, rows, lanes] = von_mises

    def copies(t):
        rows = slice(8 * t, 8 * t + 8)
        place = (pl.ds(first, count), rows)
        return [
            pltpu.make_async_copy(d_buf.at[:, rows], damage.at[place], sem.at[0, t]),
            pltpu.make_async_copy(m_buf.at[:, rows], mises.at[place], sem.at[1, t]),
        ]

    for t in range(4):

        def half(k, carry, t=t):
            step(2 * t + k)
            return carry

        lax.fori_loop(0, 2, half, 0)
        for copy in copies(t):
            copy.start()
    for t in range(4):
        for copy in copies(t):
            copy.wait()


def finish_most_kernel(
    table, odd, field, near, inverse, history, stress, labels, damage, mises, d_buf, m_buf, sem
):
    is_odd, shift = odd[0] == 1, 8 * odd[0]

    def window(w, rows, lanes):
        if w < 8:
            return jnp.where(is_odd, near[w, rows, lanes], field[w, rows, lanes])
        if w < 32:
            return field[w - shift, rows, lanes]
        return jnp.where(is_odd, field[w - 8, rows, lanes], near[w - 32, rows, lanes])

    first = 8 - shift
    finish_planes(
        table, window, 24, first, inverse, history, stress, labels, d_buf, m_buf, damage, mises, sem
    )


def finish_rest_kernel(
    table, odd, field, far, inverse, history, stress, labels, d_in, m_in, damage, mises, d_buf, m_buf, sem
):
    del d_in, m_in
    is_odd, shift = odd[0] == 1, 8 * odd[0]

    def window(w, rows, lanes):
        if w < 8:
            return jnp.where(is_odd, field[16 + w, rows, lanes], far[w, rows, lanes])
        if w < 16:
            return field[w - 8 + 3 * shift, rows, lanes]
        return jnp.where(is_odd, far[w - 16, rows, lanes], field[w - 8, rows, lanes])

    first = 3 * shift
    finish_planes(
        table, window, 8, first, inverse, history, stress, labels, d_buf, m_buf, damage, mises, sem
    )


def shards(
    displacement,
    applied_strain,
    labels,
    history,
    modulus,
    poisson,
    threshold,
    ductility,
    brittleness,
    weight,
):
    (table,) = call(
        table_kernel, [(8, 4)], n_in=6, smem=range(6), out_spaces=[pltpu.SMEM], limit=1 << 20
    )(modulus, poisson, threshold, ductility, brittleness, weight)
    gz = jnp.stack([jnp.asarray(m) for m in split_const(band(256, 256, 0).T)])
    low, high = band(256, 8, -8).T, band(256, 8, 256).T
    own = band(256, 256, 0).T[255:256]
    h_hi, h_lo = split_const(np.concatenate([low, high, own, np.zeros((7, 256))], axis=0))
    gh = jnp.asarray(np.concatenate([h_hi, h_hi, h_lo], axis=0))
    y_hi, y_lo = split_const(band(32, 48, -8))
    gy = jnp.asarray(np.concatenate([y_hi, y_hi, y_lo], axis=1))

    field3, edge_x, edge_y = (32, 32, 256), (8, 32, 256), (32, 8, 256)
    hbm, vmem, dma = pltpu.HBM, pltpu.VMEM, pltpu.SemaphoreType.DMA
    xm, ym, displacement = call(
        planes_kernel, [(3, 32, 256), (3, 32, 256), displacement.shape], scratch=[dma((1,))]
    )(displacement)
    x_token = xm
    xm = shift_route(xm, ("gx",), (-1,))
    near, far = call(
        weight_edges_kernel, [edge_x, edge_x], spaces=[None, hbm],
        scratch=[vmem(edge_x, jnp.int32), vmem(edge_x, jnp.int32), dma((2,))], smem=(0,), odd=1,
        after=(x_token,),
    )(weight, labels)
    w_near, w_far = swap_route(near, "gx", 0), swap_route(far, "gx", 1)
    (ym,) = call(extend_kernel, [(3, 40, 256)], n_in=2, after=(near,))(ym, xm)
    y_token = ym
    ym = shift_route(ym, ("gy",), (-1,))
    (nodes,) = call(columns_kernel, [(96, 128)], n_in=2, after=(y_token,))(displacement, labels)
    top, second = call(strain_kernel, [field3, field3], n_in=6, smem=(0, 1))(
        table, applied_strain, displacement, xm, ym, labels
    )
    (mine,) = call(zpack_kernel, [(240, 128)], n_in=4)(top, nodes, xm, ym)
    peer = shift_route(mine, ("gz",), (1,))
    weights, near, far = call(
        weights_x_kernel, [field3, edge_y, edge_y], n_in=4, smem=(0,), odd=1, after=(mine,)
    )(table, labels, w_near, w_far)
    w_near, w_far = swap_route(near, "gy", 0), swap_route(far, "gy", 1)
    (local,) = call(z_local_kernel, [field3], n_in=2, after=(near,))(top, gz)
    top, near, far, second_last = call(
        top_z_kernel, [field3, edge_y, edge_y, (32, 128)], scratch=[vmem((32, 128), F32)], n_in=6, smem=(0, 1), odd=2
    )(table, applied_strain, local, mine, peer, gh)
    t_near, t_far = swap_route(near, "gy", 0), swap_route(far, "gy", 1)
    weights, cols = call(
        weights_y_kernel, [field3, (128, 128)], n_in=5, odd=0, after=(near,)
    )(weights, w_near, w_far, gy, gz)
    z_token = cols
    cols = shift_route(cols, ("gz",), (1,))
    (stress,) = call(stress_kernel, [field3], n_in=4, smem=(0,), after=(z_token,))(table, labels, second, second_last)
    top, near, far = call(top_y_kernel, [field3, edge_x, edge_x], n_in=4, odd=0, after=(stress,))(
        top, t_near, t_far, gy
    )
    (inverse,) = call(weights_z_kernel, [field3], n_in=3, after=(near,))(weights, cols, gh)
    near, far = swap_route(near, "gx", 0), swap_route(far, "gx", 1)
    outs = [field3, field3]
    damage, mises = call(
        finish_most_kernel, outs, n_in=7, smem=(0,), odd=1, out_spaces=[hbm, hbm],
        scratch=[vmem((24, 32, 256), F32), vmem((24, 32, 256), F32), dma((2, 4))],
    )(table, top, near, inverse, history, stress, labels)
    return call(
        finish_rest_kernel, outs, smem=(0,), odd=1, out_spaces=[hbm, hbm],
        spaces=[None] * 7 + [hbm, hbm], aliases={7: 0, 8: 1},
        scratch=[vmem((8, 32, 256), F32), vmem((8, 32, 256), F32), dma((2, 4))],
    )(table, top, far, inverse, history, stress, labels, damage, mises)


def solution(mesh):
    cells = P("gx", "gy", "gz")
    placed = (P(None, "gx", "gy", "gz"), P(), cells, cells, P(), P(), P(), P(), P(), P())

    def body(*args):
        return tuple(shards(*args))

    return jax.shard_map(
        body, mesh=mesh, in_specs=placed, out_specs=(cells, cells), check_vma=False
    )
```

profile of v0, /device:TPU:32, one launch (start us, length us, event | category | flops | bytes accessed | tf_op | source)
XLA Modules:
  0.0 68.9 jit_solution(1319633204362753781)
XLA Ops:
  0.6 0.0 copy-start
  0.6 0.0 copy-start.2
  0.7 2.0 %copy-done.2 = f32[3,32,32,256]{3,2,1,0:T(8,128)S(1)} copy-done((f32[3,32,32,256]{3,2,1,0:T(8,128)S(1)}, f32[3,32,32,256]{3,2,1,0:T(8,128)}, u32[]{:S(2)}) %copy-start.2) | copy-done | bytes 3145752
  2.6 0.0 copy-start.6
  2.6 0.0 copy-start.8
  2.6 0.0 copy-start.9
  2.6 0.0 copy-start.10
  2.6 0.0 copy-start.11
  2.6 0.0 copy-start.12
  2.7 0.3 shard_map.150
  2.9 0.0 copy-start.7
  3.0 0.1 collective-permute-start
  3.0 0.0 copy-done
  3.1 0.3 copy-done.6
  3.3 0.7 %shard_map.151 = (f32[8,32,256]{2,1,0:T(8,128)S(1)}, f32[8,32,256]{2,1,0:T(8,128)S(1)}) custom-call(f32[4]{0:T(128)S(1)} %copy-done.6, s32[32,32,256]{2,1,0:T(8,128)S(1)} %copy-done, f32[3,32,256]{2,1,0:T(8,128)S(1)} %get-tuple-element.24.refs_2_), custom_call_target="tpu_custom_call" | custom-call | tf_op jit(solution)/shard_map/pallas_call | solution.py:94
  4.1 1.7 %collective-permute-start.3 = (f32[8,32,256]{2,1,0:T(8,128)S(1)}, f32[8,32,256]{2,1,0:T(8,128)S(1)}, u32[]{:S(2)}, u32[]{:S(2)}) collective-permute-start(f32[8,32,256]{2,1,0:T(8,128)S(1)} %get-tuple-element.28), channel_id=1, source_target_pairs={{32,64},{64,32},{96,128},{128,96},{160,192},{192,160},{224,0},{0,2... | collective-permute-start | bytes 786440 | tf_op jit(solution)/shard_map/ppermute | solution.py:65
  5.8 0.4 collective-permute-start.2
  6.2 0.0 collective-permute-done.refs_1_.refs_3_.refs_2_
  6.2 5.3 %collective-permute-start.1 = (f32[3,40,256]{2,1,0:T(8,128)S(1)}, f32[3,40,256]{2,1,0:T(8,128)S(1)}, u32[]{:S(2)}, u32[]{:S(2)}) collective-permute-start(f32[3,40,256]{2,1,0:T(8,128)S(1)} %shard_map.152.refs_2_), channel_id=1, source_target_pairs={{0,30},{2,0},{4,2},{6,4},{8,6},{10,8},{12,10},{14,12},{16,14},{18,... | collective-permute-start | bytes 368648 | tf_op jit(solution)/shard_map/ppermute | solution.py:56
  11.5 0.0 copy-done.8
  11.5 0.0 copy-done.9
  11.5 0.0 copy-done.10
  11.5 0.0 copy-done.11
  11.5 0.0 copy-done.12
  11.5 1.3 %shard_map.149.refs_0_ = f32[8,4]{1,0:T(8,128)S(1)} custom-call(f32[4]{0:T(128)S(1)} %copy-done.8, f32[4]{0:T(128)S(1)} %copy-done.9, f32[4]{0:T(128)S(1)} %copy-done.10, f32[4]{0:T(128)S(1)} %copy-done.11, f32[4]{0:T(128)S(1)} %copy-done.12, f32[4]{0:T(128)S(1)} %copy-done.6), custom_call_target="tpu_custom_call" | custom-call | tf_op jit(solution)/shard_map/pallas_call | solution.py:94
  12.8 2.0 %shard_map.154.refs_1_ = f32[96,128]{1,0:T(8,128)S(1)} custom-call(f32[3,32,32,256]{3,2,1,0:T(8,128)S(1)} %get-tuple-element.23.refs_2_.refs_0_, s32[32,32,256]{2,1,0:T(8,128)S(1)} %copy-done, f32[3,40,256]{2,1,0:T(8,128)S(1)} %shard_map.152.refs_2_), custom_call_target="tpu_custom_call" | custom-call | tf_op jit(solution)/shard_map/pallas_call | solution.py:94
  14.8 0.0 copy-start.3
  14.9 0.0 collective-permute-done.1.refs_4_.refs_3_
  14.9 0.0 copy-done.7
  14.9 5.5 %shard_map.153 = (f32[32,32,256]{2,1,0:T(8,128)S(1)}, f32[32,32,256]{2,1,0:T(8,128)S(1)}) custom-call(f32[8,4]{1,0:T(8,128)S(1)} %shard_map.149.refs_0_, f32[6]{0:T(128)S(1)} %copy-done.7, f32[3,32,32,256]{3,2,1,0:T(8,128)S(1)} %get-tuple-element.23.refs_2_.refs_0_, f32[3,32,256]{2,1,0:T(8,128)S(1)} %collective-permute-done.refs_1_.refs_3_.refs_2_, ...), custom_call_target="tpu_custom_call" | custom-call | tf_op jit(solution)/shard_map/pallas_call | solution.py:94
  20.4 0.0 copy-start.4
  20.4 0.6 shard_map.155.refs_4_.refs_3_
  20.9 6.0 %collective-permute-start.4 = (f32[240,128]{1,0:T(8,128)S(1)}, f32[240,128]{1,0:T(8,128)S(1)}, u32[]{:S(2)}, u32[]{:S(2)}) collective-permute-start(f32[240,128]{1,0:T(8,128)S(1)} %shard_map.155.refs_4_.refs_3_), channel_id=1, source_target_pairs={{0,1},{1,0},{2,3},{3,2},{4,5},{5,4},{6,7},{7,6},{8,9},{9,8},{10,11... | collective-permute-start | bytes 368648 | tf_op jit(solution)/shard_map/ppermute | solution.py:56
  26.9 0.0 collective-permute-done.3.refs_3_
  26.9 0.0 collective-permute-done.2.refs_2_
  26.9 1.9 %shard_map.156 = (f32[32,32,256]{2,1,0:T(8,128)S(1)}, f32[32,8,256]{2,1,0:T(8,128)S(1)}, f32[32,8,256]{2,1,0:T(8,128)S(1)}) custom-call(f32[8,4]{1,0:T(8,128)S(1)} %shard_map.149.refs_0_, s32[32,32,256]{2,1,0:T(8,128)S(1)} %copy-done, f32[8,32,256]{2,1,0:T(8,128)S(1)} %collective-permute-done.2.refs_2_, f32[8,32,256]{2,1,0:T(8,128)S(1)} %collective-permute-done.3.refs_3_, ...), custom_call_target="tpu_custom_call" | custom-call | tf_op jit(solution)/shard_map/pallas_call | solution.py:94
  28.8 5.9 %collective-permute-start.8 = (f32[32,8,256]{2,1,0:T(8,128)S(1)}, f32[32,8,256]{2,1,0:T(8,128)S(1)}, u32[]{:S(2)}, u32[]{:S(2)}) collective-permute-start(f32[32,8,256]{2,1,0:T(8,128)S(1)} %get-tuple-element.36), channel_id=1, source_target_pairs={{2,4},{4,2},{6,8},{8,6},{10,12},{12,10},{14,16},{16,14},{18,20},{2... | collective-permute-start | bytes 786440 | tf_op jit(solution)/shard_map/ppermute | solution.py:65
  34.6 0.0 collective-permute-start.7
  34.6 0.0 copy-done.3
  34.7 0.6 shard_map.157.refs_2_
  35.2 0.0 collective-permute-done.4.refs_4_
  35.2 0.0 copy-done.4
  35.3 1.6 %shard_map.158 = (f32[32,32,256]{2,1,0:T(8,128)S(1)}, f32[32,8,256]{2,1,0:T(8,128)S(1)}, f32[32,8,256]{2,1,0:T(8,128)S(1)}, f32[32,128]{1,0:T(8,128)S(1)}) custom-call(f32[8,4]{1,0:T(8,128)S(1)} %shard_map.149.refs_0_, f32[6]{0:T(128)S(1)} %copy-done.7, f32[32,32,256]{2,1,0:T(8,128)S(1)} %shard_map.157.refs_2_, f32[240,128]{1,0:T(8,128)S(1)} %shard_map.155.refs_4_.refs_3_, ...), custom_call_target="tpu_custom_call" | custom-call | tf_op jit(solution)/shard_map/pallas_call | solution.py:94
  36.8 1.1 %collective-permute-start.6 = (f32[32,8,256]{2,1,0:T(8,128)S(1)}, f32[32,8,256]{2,1,0:T(8,128)S(1)}, u32[]{:S(2)}, u32[]{:S(2)}) collective-permute-start(f32[32,8,256]{2,1,0:T(8,128)S(1)} %get-tuple-element.32), channel_id=1, source_target_pairs={{2,4},{4,2},{6,8},{8,6},{10,12},{12,10},{14,16},{16,14},{18,20},{2... | collective-permute-start | bytes 786440 | tf_op jit(solution)/shard_map/ppermute | solution.py:65
  37.9 1.1 %collective-permute-start.5 = (f32[32,8,256]{2,1,0:T(8,128)S(1)}, f32[32,8,256]{2,1,0:T(8,128)S(1)}, u32[]{:S(2)}, u32[]{:S(2)}) collective-permute-start(f32[32,8,256]{2,1,0:T(8,128)S(1)} %get-tuple-element.31.refs_5_), channel_id=1, source_target_pairs={{0,2},{2,0},{4,6},{6,4},{8,10},{10,8},{12,14},{14,12},{16,18},{18,... | collective-permute-start | bytes 786440 | tf_op jit(solution)/shard_map/ppermute | solution.py:65
  39.0 2.3 %collective-permute-done.8.refs_2_ = f32[32,8,256]{2,1,0:T(8,128)S(1)} collective-permute-done((f32[32,8,256]{2,1,0:T(8,128)S(1)}, f32[32,8,256]{2,1,0:T(8,128)S(1)}, u32[]{:S(2)}, u32[]{:S(2)}) %collective-permute-start.8) | collective-permute-done | bytes 262176 | tf_op jit(solution)/shard_map/ppermute | solution.py:65
  41.3 2.5 %collective-permute-done.7.refs_1_ = f32[32,8,256]{2,1,0:T(8,128)S(1)} collective-permute-done((f32[32,8,256]{2,1,0:T(8,128)S(1)}, f32[32,8,256]{2,1,0:T(8,128)S(1)}, u32[]{:S(2)}, u32[]{:S(2)}) %collective-permute-start.7) | collective-permute-done | bytes 262176 | tf_op jit(solution)/shard_map/ppermute | solution.py:65
  43.8 0.0 copy-done.5
  43.8 1.5 %shard_map.159 = (f32[32,32,256]{2,1,0:T(8,128)S(1)}, f32[128,128]{1,0:T(8,128)S(1)}) custom-call(f32[32,32,256]{2,1,0:T(8,128)S(1)} %get-tuple-element.35.refs_0_, f32[32,8,256]{2,1,0:T(8,128)S(1)} %collective-permute-done.7.refs_1_, f32[32,8,256]{2,1,0:T(8,128)S(1)} %collective-permute-done.8.refs_2_, bf16[32,144]{1,0:T(8,128)(2,1)S(1)} %copy-done.5, ...), custom_call_target="tpu_custom_call" | custom-call | tf_op jit(solution)/shard_map/pallas_call | solution.py:94
  45.3 2.0 %shard_map.160.refs_4_.refs_5_ = f32[32,32,256]{2,1,0:T(8,128)S(1)} custom-call(f32[8,4]{1,0:T(8,128)S(1)} %shard_map.149.refs_0_, s32[32,32,256]{2,1,0:T(8,128)S(1)} %copy-done, f32[32,32,256]{2,1,0:T(8,128)S(1)} %get-tuple-element.33.refs_2_, f32[32,128]{1,0:T(8,128)S(1)} %get-tuple-element.34.refs_3_, f32[128,128]{1,0:T(8,128)S(1)} %get-tuple-element.37.refs_4_), custom_call_target="tpu_custom_call" | custom-call | tf_op jit(solution)/shard_map/pallas_call | solution.py:94
  47.3 0.0 copy-start.1
  47.3 0.7 %collective-permute-done.6.refs_2_ = f32[32,8,256]{2,1,0:T(8,128)S(1)} collective-permute-done((f32[32,8,256]{2,1,0:T(8,128)S(1)}, f32[32,8,256]{2,1,0:T(8,128)S(1)}, u32[]{:S(2)}, u32[]{:S(2)}) %collective-permute-start.6) | collective-permute-done | bytes 262176 | tf_op jit(solution)/shard_map/ppermute | solution.py:65
  48.0 0.0 collective-permute-done.5.refs_1_
  48.0 0.9 %shard_map.161 = (f32[32,32,256]{2,1,0:T(8,128)S(1)}, f32[8,32,256]{2,1,0:T(8,128)S(1)}, f32[8,32,256]{2,1,0:T(8,128)S(1)}) custom-call(f32[32,32,256]{2,1,0:T(8,128)S(1)} %get-tuple-element.30.refs_0_, f32[32,8,256]{2,1,0:T(8,128)S(1)} %collective-permute-done.5.refs_1_, f32[32,8,256]{2,1,0:T(8,128)S(1)} %collective-permute-done.6.refs_2_, ...), custom_call_target="tpu_custom_call" | custom-call | tf_op jit(solution)/shard_map/pallas_call | solution.py:94
  49.0 0.1 collective-permute-start.11
  49.1 0.8 %collective-permute-start.9 = (f32[8,32,256]{2,1,0:T(8,128)S(1)}, f32[8,32,256]{2,1,0:T(8,128)S(1)}, u32[]{:S(2)}, u32[]{:S(2)}) collective-permute-start(f32[8,32,256]{2,1,0:T(8,128)S(1)} %get-tuple-element.39), channel_id=1, source_target_pairs={{32,64},{64,32},{96,128},{128,96},{160,192},{192,160},{224,0},{0,2... | collective-permute-start | bytes 786440 | tf_op jit(solution)/shard_map/ppermute | solution.py:65
  49.8 4.0 %collective-permute-start.10 = (f32[128,128]{1,0:T(8,128)S(1)}, f32[128,128]{1,0:T(8,128)S(1)}, u32[]{:S(2)}, u32[]{:S(2)}) collective-permute-start(f32[128,128]{1,0:T(8,128)S(1)} %get-tuple-element.37.refs_4_), channel_id=1, source_target_pairs={{0,1},{1,0},{2,3},{3,2},{4,5},{5,4},{6,7},{7,6},{8,9},{9,8},{10,11... | collective-permute-start | bytes 196616 | tf_op jit(solution)/shard_map/ppermute | solution.py:56
  53.9 9.2 %collective-permute-done.10.refs_1_ = f32[128,128]{1,0:T(8,128)S(1)} collective-permute-done((f32[128,128]{1,0:T(8,128)S(1)}, f32[128,128]{1,0:T(8,128)S(1)}, u32[]{:S(2)}, u32[]{:S(2)}) %collective-permute-start.10) | collective-permute-done | bytes 65568 | tf_op jit(solution)/shard_map/ppermute | solution.py:56
  63.0 0.6 shard_map.162.refs_3_
  63.6 0.0 collective-permute-done.11.refs_2_
  63.7 0.0 copy-done.1
  63.7 3.2 %shard_map.163 = (f32[32,32,256]{2,1,0:T(8,128)}, f32[32,32,256]{2,1,0:T(8,128)}) custom-call(f32[8,4]{1,0:T(8,128)S(1)} %shard_map.149.refs_0_, f32[32,32,256]{2,1,0:T(8,128)S(1)} %get-tuple-element.38.refs_1_, f32[8,32,256]{2,1,0:T(8,128)S(1)} %collective-permute-done.11.refs_2_, f32[32,32,256]{2,1,0:T(8,128)S(1)} %shard_map.162.refs_3_, ...), custom_call_target="tpu_custom_call" | custom-call | tf_op jit(solution)/shard_map/pallas_call | solution.py:94
  66.8 0.0 collective-permute-done.9.refs_2_
  66.9 2.1 %shard_map.164 = (f32[32,32,256]{2,1,0:T(8,128)}, f32[32,32,256]{2,1,0:T(8,128)}) custom-call(f32[8,4]{1,0:T(8,128)S(1)} %shard_map.149.refs_0_, f32[32,32,256]{2,1,0:T(8,128)S(1)} %get-tuple-element.38.refs_1_, f32[8,32,256]{2,1,0:T(8,128)S(1)} %collective-permute-done.9.refs_2_, ...), custom_call_target="tpu_custom_call", output_to_operand_aliasing={{0}: (7, {}), {1}: (8, {})} | custom-call | tf_op jit(solution)/shard_map/pallas_call | solution.py:94
  (2 shorter events, 0.0 us)
Async XLA Ops:
  0.6 2.4 %copy-start = (s32[32,32,256]{2,1,0:T(8,128)S(1)}, s32[32,32,256]{2,1,0:T(8,128)}, u32[]{:S(2)}) copy-start(s32[32,32,256]{2,1,0:T(8,128)} %refs_6_.3) | copy-start | bytes 3145732
  0.6 2.0 %copy-start.2 = (f32[3,32,32,256]{3,2,1,0:T(8,128)S(1)}, f32[3,32,32,256]{3,2,1,0:T(8,128)}, u32[]{:S(2)}) copy-start(f32[3,32,32,256]{3,2,1,0:T(8,128)} %refs_0_.4) | copy-start | bytes 9437188
  2.6 0.7 %copy-start.6 = (f32[4]{0:T(128)S(1)}, f32[4]{0:T(128)}, u32[]{:S(2)}) copy-start(f32[4]{0:T(128)} %refs_0_.5) | copy-start | bytes 52
  2.6 8.9 %copy-start.8 = (f32[4]{0:T(128)S(1)}, f32[4]{0:T(128)}, u32[]{:S(2)}) copy-start(f32[4]{0:T(128)} %refs_0_.3) | copy-start | bytes 52
  2.6 8.9 %copy-start.9 = (f32[4]{0:T(128)S(1)}, f32[4]{0:T(128)}, u32[]{:S(2)}) copy-start(f32[4]{0:T(128)} %refs_1_.7) | copy-start | bytes 52
  2.6 8.9 %copy-start.10 = (f32[4]{0:T(128)S(1)}, f32[4]{0:T(128)}, u32[]{:S(2)}) copy-start(f32[4]{0:T(128)} %refs_2_.2) | copy-start | bytes 52
  2.6 8.9 %copy-start.11 = (f32[4]{0:T(128)S(1)}, f32[4]{0:T(128)}, u32[]{:S(2)}) copy-start(f32[4]{0:T(128)} %refs_3_.3) | copy-start | bytes 52
  2.6 8.9 %copy-start.12 = (f32[4]{0:T(128)S(1)}, f32[4]{0:T(128)}, u32[]{:S(2)}) copy-start(f32[4]{0:T(128)} %refs_4_.3) | copy-start | bytes 52
  2.9 11.9 %copy-start.7 = (f32[6]{0:T(128)S(1)}, f32[6]{0:T(128)}, u32[]{:S(2)}) copy-start(f32[6]{0:T(128)} %refs_1_.12) | copy-start | bytes 76
  3.0 3.2 %collective-permute-start = (f32[3,32,256]{2,1,0:T(8,128)S(1)}, f32[3,32,256]{2,1,0:T(8,128)S(1)}, u32[]{:S(2)}, u32[]{:S(2)}) collective-permute-start(f32[3,32,256]{2,1,0:T(8,128)S(1)} %get-tuple-element.24.refs_2_), channel_id=1, source_target_pairs={{0,224},{32,0},{64,32},{96,64},{128,96},{160,128},{192,160},{224,1... | collective-permute-start | bytes 294920 | tf_op jit(solution)/shard_map/ppermute | solution.py:56
  4.1 22.8 %collective-permute-start.3 = (f32[8,32,256]{2,1,0:T(8,128)S(1)}, f32[8,32,256]{2,1,0:T(8,128)S(1)}, u32[]{:S(2)}, u32[]{:S(2)}) collective-permute-start(f32[8,32,256]{2,1,0:T(8,128)S(1)} %get-tuple-element.28), channel_id=1, source_target_pairs={{32,64},{64,32},{96,128},{128,96},{160,192},{192,160},{224,0},{0,2... | collective-permute-start | bytes 786440 | tf_op jit(solution)/shard_map/ppermute | solution.py:65
  5.8 21.1 %collective-permute-start.2 = (f32[8,32,256]{2,1,0:T(8,128)S(1)}, f32[8,32,256]{2,1,0:T(8,128)S(1)}, u32[]{:S(2)}, u32[]{:S(2)}) collective-permute-start(f32[8,32,256]{2,1,0:T(8,128)S(1)} %get-tuple-element.26.refs_2_), channel_id=1, source_target_pairs={{0,32},{32,0},{64,96},{96,64},{128,160},{160,128},{192,224},{224,1... | collective-permute-start | bytes 786440 | tf_op jit(solution)/shard_map/ppermute | solution.py:65
  6.2 8.7 %collective-permute-start.1 = (f32[3,40,256]{2,1,0:T(8,128)S(1)}, f32[3,40,256]{2,1,0:T(8,128)S(1)}, u32[]{:S(2)}, u32[]{:S(2)}) collective-permute-start(f32[3,40,256]{2,1,0:T(8,128)S(1)} %shard_map.152.refs_2_), channel_id=1, source_target_pairs={{0,30},{2,0},{4,2},{6,4},{8,6},{10,8},{12,10},{14,12},{16,14},{18,... | collective-permute-start | bytes 368648 | tf_op jit(solution)/shard_map/ppermute | solution.py:56
  14.8 19.8 %copy-start.3 = (bf16[2,256,256]{2,1,0:T(8,128)(2,1)S(1)}, bf16[2,256,256]{2,1,0:T(8,128)(2,1)}, u32[]{:S(2)}) copy-start(bf16[2,256,256]{2,1,0:T(8,128)(2,1)} %constant.14.refs_1_.refs_4_) | copy-start | bytes 786436
  20.4 14.9 %copy-start.4 = (bf16[72,256]{1,0:T(8,128)(2,1)S(1)}, bf16[72,256]{1,0:T(8,128)(2,1)}, u32[]{:S(2)}) copy-start(bf16[72,256]{1,0:T(8,128)(2,1)} %constant.10.clone.refs_5_.refs_2_) | copy-start | bytes 110596
  20.9 22.9 %copy-start.5 = (bf16[32,144]{1,0:T(8,128)(2,1)S(1)}, bf16[32,144]{1,0:T(8,128)(2,1)}, u32[]{:S(2)}) copy-start(bf16[32,144]{1,0:T(8,128)(2,1)} %constant.11.clone.refs_3_) | copy-start | bytes 27652
  20.9 14.3 %collective-permute-start.4 = (f32[240,128]{1,0:T(8,128)S(1)}, f32[240,128]{1,0:T(8,128)S(1)}, u32[]{:S(2)}, u32[]{:S(2)}) collective-permute-start(f32[240,128]{1,0:T(8,128)S(1)} %shard_map.155.refs_4_.refs_3_), channel_id=1, source_target_pairs={{0,1},{1,0},{2,3},{3,2},{4,5},{5,4},{6,7},{7,6},{8,9},{9,8},{10,11... | collective-permute-start | bytes 368648 | tf_op jit(solution)/shard_map/ppermute | solution.py:56
  28.8 12.6 %collective-permute-start.8 = (f32[32,8,256]{2,1,0:T(8,128)S(1)}, f32[32,8,256]{2,1,0:T(8,128)S(1)}, u32[]{:S(2)}, u32[]{:S(2)}) collective-permute-start(f32[32,8,256]{2,1,0:T(8,128)S(1)} %get-tuple-element.36), channel_id=1, source_target_pairs={{2,4},{4,2},{6,8},{8,6},{10,12},{12,10},{14,16},{16,14},{18,20},{2... | collective-permute-start | bytes 786440 | tf_op jit(solution)/shard_map/ppermute | solution.py:65
  34.6 9.2 %collective-permute-start.7 = (f32[32,8,256]{2,1,0:T(8,128)S(1)}, f32[32,8,256]{2,1,0:T(8,128)S(1)}, u32[]{:S(2)}, u32[]{:S(2)}) collective-permute-start(f32[32,8,256]{2,1,0:T(8,128)S(1)} %get-tuple-element.29.refs_2_), channel_id=1, source_target_pairs={{0,2},{2,0},{4,6},{6,4},{8,10},{10,8},{12,14},{14,12},{16,18},{18,... | collective-permute-start | bytes 786440 | tf_op jit(solution)/shard_map/ppermute | solution.py:65
  36.8 11.2 %collective-permute-start.6 = (f32[32,8,256]{2,1,0:T(8,128)S(1)}, f32[32,8,256]{2,1,0:T(8,128)S(1)}, u32[]{:S(2)}, u32[]{:S(2)}) collective-permute-start(f32[32,8,256]{2,1,0:T(8,128)S(1)} %get-tuple-element.32), channel_id=1, source_target_pairs={{2,4},{4,2},{6,8},{8,6},{10,12},{12,10},{14,16},{16,14},{18,20},{2... | collective-permute-start | bytes 786440 | tf_op jit(solution)/shard_map/ppermute | solution.py:65
  37.9 10.1 %collective-permute-start.5 = (f32[32,8,256]{2,1,0:T(8,128)S(1)}, f32[32,8,256]{2,1,0:T(8,128)S(1)}, u32[]{:S(2)}, u32[]{:S(2)}) collective-permute-start(f32[32,8,256]{2,1,0:T(8,128)S(1)} %get-tuple-element.31.refs_5_), channel_id=1, source_target_pairs={{0,2},{2,0},{4,6},{6,4},{8,10},{10,8},{12,14},{14,12},{16,18},{18,... | collective-permute-start | bytes 786440 | tf_op jit(solution)/shard_map/ppermute | solution.py:65
  47.3 16.4 %copy-start.1 = (f32[32,32,256]{2,1,0:T(8,128)S(1)}, f32[32,32,256]{2,1,0:T(8,128)}, u32[]{:S(2)}) copy-start(f32[32,32,256]{2,1,0:T(8,128)} %refs_4_.5) | copy-start | bytes 3145732
  49.0 14.7 %collective-permute-start.11 = (f32[8,32,256]{2,1,0:T(8,128)S(1)}, f32[8,32,256]{2,1,0:T(8,128)S(1)}, u32[]{:S(2)}, u32[]{:S(2)}) collective-permute-start(f32[8,32,256]{2,1,0:T(8,128)S(1)} %get-tuple-element.41.refs_3_), channel_id=1, source_target_pairs={{0,32},{32,0},{64,96},{96,64},{128,160},{160,128},{192,224},{224,1... | collective-permute-start | bytes 786440 | tf_op jit(solution)/shard_map/ppermute | solution.py:65
  49.1 17.8 %collective-permute-start.9 = (f32[8,32,256]{2,1,0:T(8,128)S(1)}, f32[8,32,256]{2,1,0:T(8,128)S(1)}, u32[]{:S(2)}, u32[]{:S(2)}) collective-permute-start(f32[8,32,256]{2,1,0:T(8,128)S(1)} %get-tuple-element.39), channel_id=1, source_target_pairs={{32,64},{64,32},{96,128},{128,96},{160,192},{192,160},{224,0},{0,2... | collective-permute-start | bytes 786440 | tf_op jit(solution)/shard_map/ppermute | solution.py:65
  49.8 13.2 %collective-permute-start.10 = (f32[128,128]{1,0:T(8,128)S(1)}, f32[128,128]{1,0:T(8,128)S(1)}, u32[]{:S(2)}, u32[]{:S(2)}) collective-permute-start(f32[128,128]{1,0:T(8,128)S(1)} %get-tuple-element.37.refs_4_), channel_id=1, source_target_pairs={{0,1},{1,0},{2,3},{3,2},{4,5},{5,4},{6,7},{7,6},{8,9},{9,8},{10,11... | collective-permute-start | bytes 196616 | tf_op jit(solution)/shard_map/ppermute | solution.py:56
where the time goes:
time: 69.9 us; the launch traced here: 68.9 us
  starting transfers between devices  26.4 us (38%)
  Pallas kernels  24.6 us (35%)
  waiting for transfers between devices  14.7 us (21%)
  local copies, waits for them, and re-layouts  2.3 us (3%)
  between operations  0.91 us (1%)
    pallas_call x16, Pallas kernels, call(): return lambda *args: built(*args, *after)  24.6 us
    ppermute x4, starting transfers between devices, shift_route(): return lax.ppermute(block, axes if len(axes) > 1 else axes[0], route)  15.3 us
    ppermute x8, starting transfers between devices, swap_route(): return lax.ppermute(block, axis, route)  11.1 us
    ppermute x4, waiting for transfers between devices, shift_route(): return lax.ppermute(block, axes if len(axes) > 1 else axes[0], route)  9.17 us
    ppermute x8, waiting for transfers between devices, swap_route(): return lax.ppermute(block, axis, route)  5.55 us
    unnamed x26, local copies, waits for them, and re-layouts  2.3 us
  transfers between devices with their start and end apart: 12, of which 4 were waited for; matrix products, arithmetic and copies ran while one was open for 0% of the time, Pallas kernels for 31%

commit v1 on v0

--- a/solution.py
+++ b/solution.py
@@ -94,10 +94,14 @@
     return lambda *args: built(*args, *after)
 
 
-def pick(labels, table, row):
-    out = jnp.where(labels == 0, table[row, 0], table[row, 3])
-    out = jnp.where(labels == 1, table[row, 1], out)
-    return jnp.where(labels == 2, table[row, 2], out)
+def pick(labels, entries):
+    out = jnp.where(labels == 0, entries[0], entries[3])
+    out = jnp.where(labels == 1, entries[1], out)
+    return jnp.where(labels == 2, entries[2], out)
+
+
+def each(fn, *params):
+    return [fn(*(p[k] for p in params)) for k in range(4)]
 
 
 def edge_columns(field, put):
@@ -105,34 +109,15 @@
         put(j, field(j, 0).T[0:8], field(j, 1).T[120:128])
 
 
-def table_kernel(modulus, poisson, threshold, ductility, brittleness, weight, table):
-    for k in range(4):
-        nu, w = poisson[k], weight[k]
-        lead, shear = 1.0 - 2.0 * nu, 1.0 / (1.0 + nu)
-        table[0, k] = 0.45 * w / lead
-        table[1, k] = 0.3 * (w * shear) * (w * shear)
-        table[2, k] = w
-        table[3, k] = math.sqrt(3.0) * modulus[k] * shear
-        table[4, k] = threshold[k]
-        table[5, k] = threshold[k] * (1.0 - ductility[k])
-        table[6, k] = ductility[k]
-        table[7, k] = brittleness[k]
-
-
-def planes_kernel(u, xm, ym, kept, sem):
+def planes_kernel(u, xm, ym, xym, kept, sem):
     keep = pltpu.make_async_copy(u, kept, sem.at[0])
     keep.start()
     for c in range(3):
         xm[c] = u[c, 0]
         for x in range(32):
             ym[c, x : x + 1, :] = u[c, x, 0:1, :]
+        xym[c : c + 1, :] = u[c, 0, 0:1, :]
     keep.wait()
-
-
-def extend_kernel(ym, xm, out):
-    for c in range(3):
-        out[c, 0:32] = ym[c]
-        out[c, 32:33, :] = xm[c, 0:1, :]
 
 
 def weight_edges_kernel(weight, odd, labels, near, far, low, high, sem):
@@ -146,13 +131,8 @@
         copy.wait()
     is_odd = odd[0] == 1
 
-    def choose(lab):
-        w = jnp.where(lab == 0, weight[0], weight[3])
-        w = jnp.where(lab == 1, weight[1], w)
-        return jnp.where(lab == 2, weight[2], w)
-
     def step(i, carry):
-        a, b = choose(low[i]), choose(high[i])
+        a, b = pick(low[i], weight), pick(high[i], weight)
         near[i] = jnp.where(is_odd, a, b)
         far[i] = jnp.where(is_odd, b, a)
         return carry
@@ -174,7 +154,7 @@
 
     zero = jnp.zeros((32, 128), F32)
     first, last, lab = lax.fori_loop(
-        0, 32, step, (zero, zero, jnp.zeros((32, 128), jnp.int32)), unroll=2
+        0, 32, step, (zero, zero, jnp.zeros((32, 128), jnp.int32)), unroll=8
     )
     nodes[0:32, :] = first
     nodes[32:64, :] = last
@@ -190,54 +170,71 @@
     return plus, minus
 
 
-def respond(applied, table, lab, sums):
-    xx = applied[0] + 0.25 * sums[0]
-    yy = applied[1] + 0.25 * sums[1]
-    zz = applied[2] + 0.25 * sums[2]
-    xy = applied[5] + 0.125 * sums[3]
-    yz = applied[3] + 0.125 * sums[4]
-    xz = applied[4] + 0.125 * sums[5]
+def root(t):
+    return t * lax.rsqrt(jnp.maximum(t, 1e-37))
+
+
+def response(poisson, weight):
+    lead = each(lambda nu, w: 0.1125 * w / (1.0 - 2.0 * nu), poisson, weight)
+    shear = each(lambda nu, w: w / (1.0 + nu), poisson, weight)
+    return lead, [(0.3 / 96.0) * (f * f) for f in shear]
+
+
+def respond(applied, law, lab, sums):
+    xx, yy, zz = (4.0 * applied[i] + sums[i] for i in range(3))
+    xy, yz, xz = (8.0 * applied[i] + sums[j] for i, j in ((5, 3), (3, 4), (4, 5)))
     trace = xx + yy + zz
     p, q, r = xx - yy, yy - zz, zz - xx
-    second = (p * p + q * q + r * r) * (1.0 / 6.0) + (yz * yz + xz * xz + xy * xy)
-    lead = pick(lab, table, 0) * trace
-    value = lead + jnp.sqrt(lead * lead + pick(lab, table, 1) * second)
-    return value, second
-
-
-def strain_kernel(table, applied, u, xm, ym, labels, top, second):
-    row = lax.broadcasted_iota(jnp.int32, (32, 256), 0)
-    inside = lax.broadcasted_iota(jnp.int32, (32, 256), 1) < 255
+    second = (p * p + q * q + r * r) + 1.5 * (yz * yz + xz * xz + xy * xy)
+    lead = pick(lab, law[0]) * trace
+    return lead + root(lead * lead + pick(lab, law[1]) * second), second
+
+
+def strain_kernel(weight, poisson, applied, u, xm, ym, xym, labels, top, second):
+    end = lax.broadcasted_iota(jnp.int32, (8, 256), 0) == 7
+    inside = lax.broadcasted_iota(jnp.int32, (8, 128), 1) < 127
+    law = response(poisson, weight)
 
     def cells(x, here, there, r_here, r_there):
-        d, s, dsh, ssh = [], [], [], []
-        for c in range(3):
-            d.append(there[c] - here[c])
-            s.append(there[c] + here[c])
-            dsh.append(jnp.where(row == 31, r_there[c] - r_here[c], pltpu.roll(d[c], 31, 0)))
-            ssh.append(jnp.where(row == 31, r_there[c] + r_here[c], pltpu.roll(s[c], 31, 0)))
-        plus, minus = combine(d, s, dsh, ssh)
-        shifted = [pltpu.roll(p, 255, 1) for p in plus]
-        value, second[x] = respond(
-            applied,
-            table,
-            labels[x],
-            [
-                minus[0] + shifted[0],
-                minus[1] + shifted[1],
-                shifted[3] - minus[3],
-                minus[2] + shifted[2],
-                minus[4] + shifted[4],
-                minus[5] + shifted[5],
-            ],
-        )
-        top[x] = jnp.where(inside, value, 0.0)
+        below = [
+            jnp.broadcast_to(line, (8, 256))
+            for c in range(3)
+            for line in (r_there[c] - r_here[c], r_there[c] + r_here[c])
+        ]
+        for k in (3, 2, 1, 0):
+            rows = slice(8 * k, 8 * k + 8)
+            d, s, dsh, ssh, turned = [], [], [], [], []
+            for c in range(3):
+                a, b = here(c, rows), there(c, rows)
+                d.append(b - a)
+                s.append(b + a)
+                turned += [pltpu.roll(d[c], 7, 0), pltpu.roll(s[c], 7, 0)]
+                dsh.append(jnp.where(end, below[2 * c], turned[2 * c]))
+                ssh.append(jnp.where(end, below[2 * c + 1], turned[2 * c + 1]))
+            below = turned
+            plus, minus = combine(d, s, dsh, ssh)
+            shifted = [pltpu.roll(p, 255, 1) for p in plus]
+            value, second[x, rows, :] = respond(
+                applied,
+                law,
+                labels[x, rows, :],
+                [
+                    minus[0] + shifted[0],
+                    minus[1] + shifted[1],
+                    shifted[3] - minus[3],
+                    minus[2] + shifted[2],
+                    minus[4] + shifted[4],
+                    minus[5] + shifted[5],
+                ],
+            )
+            top[x, rows, 0:128] = value[:, 0:128]
+            top[x, rows, 128:256] = jnp.where(inside, value[:, 128:256], 0.0)
 
     def step(x, carry):
         cells(
             x,
-            [u[c, x] for c in range(3)],
-            [u[c, x + 1] for c in range(3)],
+            lambda c, rows: u[c, x, rows, :],
+            lambda c, rows: u[c, x + 1, rows, :],
             [ym[c, pl.ds(x, 1), :] for c in range(3)],
             [ym[c, pl.ds(x + 1, 1), :] for c in range(3)],
         )
@@ -246,10 +243,10 @@
     lax.fori_loop(0, 31, step, 0)
     cells(
         31,
-        [u[c, 31] for c in range(3)],
-        [xm[c] for c in range(3)],
+        lambda c, rows: u[c, 31, rows, :],
+        lambda c, rows: xm[c, rows, :],
         [ym[c, 31:32, :] for c in range(3)],
-        [ym[c, 32:33, :] for c in range(3)],
+        [xym[c : c + 1, :] for c in range(3)],
     )
 
 
@@ -263,11 +260,11 @@
     )
 
 
-def zpack_kernel(top, nodes, xm, ym, out):
+def zpack_kernel(top, nodes, xm, ym, xym, out):
     columns_out(top, out, 0)
     lane = lax.broadcasted_iota(jnp.int32, (32, 128), 1)
     lane1 = lax.broadcasted_iota(jnp.int32, (8, 128), 1)
-    pad = jnp.zeros((88, 128), F32)
+    pad = jnp.zeros((96, 128), F32)
     for t in range(2):
         body = nodes[32 * t : 32 * t + 32, :]
         edge = jnp.zeros((8, 128), F32)
@@ -278,13 +275,15 @@
             turned = jnp.concatenate([ym[c, :, lanes], pad], axis=0).T
             line = turned[127:128] if t else turned[0:1]
             line = pltpu.roll(jnp.broadcast_to(line, (8, 128)), 40 * c, 1)
-            edge = jnp.where((lane1 >= 40 * c) & (lane1 <= at), line, edge)
+            corner = pltpu.roll(jnp.broadcast_to(xym[c : c + 1, lanes], (8, 128)), (at + t) % 128, 1)
+            edge = jnp.where((lane1 >= 40 * c) & (lane1 < at), line, edge)
+            edge = jnp.where(lane1 == at, corner, edge)
         out[128 + 40 * t : 160 + 40 * t, :] = body
         out[160 + 40 * t : 168 + 40 * t, :] = edge
     out[208:240, :] = nodes[64:96, :]
 
 
-def column_cells(applied, table, lower, upper, lab):
+def column_cells(applied, law, lower, upper, lab):
     parts = []
     for n in (lower, upper):
         nx = pltpu.roll(n, 127, 1)
@@ -299,7 +298,7 @@
     gz = [gz, pltpu.roll(gz, 88, 1), pltpu.roll(gz, 48, 1)]
     return respond(
         applied,
-        table,
+        law,
         lab.astype(jnp.int32),
         [gx[0], gy[1], gz[2], gx[1] + gy[0], gy[2] + gz[1], gx[2] + gz[0]],
     )
@@ -336,11 +335,12 @@
         out[4 * j : 4 * j + 4] = local[4 * j : 4 * j + 4] + part
 
 
-def top_z_kernel(table, applied, odd, local, mine, peer, gh, out, near, far, second_last, scratch):
+def top_z_kernel(weight, poisson, applied, odd, local, mine, peer, gh, out, near, far, second_last, scratch):
+    law = response(poisson, weight)
     last, second_last[...] = column_cells(
-        applied, table, mine[168:208, :], peer[128:168, :], mine[208:240, :]
-    )
-    before, _ = column_cells(applied, table, peer[168:208, :], mine[128:168, :], peer[208:240, :])
+        applied, law, mine[168:208, :], peer[128:168, :], mine[208:240, :]
+    )
+    before, _ = column_cells(applied, law, peer[168:208, :], mine[128:168, :], peer[208:240, :])
     last, before = blocks_of(last, scratch), blocks_of(before, scratch)
     z_halo(local, peer, gh, out, before, last)
     y_edges(odd, out, near, far)
@@ -380,8 +380,8 @@
     lax.fori_loop(0, 8, step, 0)
 
 
-def weights_x_kernel(table, odd, labels, r_near, r_far, out, near, far):
-    smooth_x(odd, lambda *at: pick(labels[at], table, 2), r_near, r_far, out)
+def weights_x_kernel(weight, odd, labels, r_near, r_far, out, near, far):
+    smooth_x(odd, lambda *at: pick(labels[at], weight), r_near, r_far, out)
     y_edges(odd, out, near, far)
 
 
@@ -415,34 +415,38 @@
     far[...] = out[pl.ds(24 - start, 8)]
 
 
-def stress_kernel(table, labels, second, second_last, stress):
+def phases_kernel(
+    modulus, poisson, threshold, ductility, brittleness,
+    labels, second, second_last, stress, start, lost, ductile, brittle,
+):
     lane = lax.broadcasted_iota(jnp.int32, (32, 128), 1)
+    stiff = each(lambda e, nu: math.sqrt(3.0 / 96.0) * e / (1.0 + nu), modulus, poisson)
+    gone = each(lambda k, a: k * (1.0 - a), threshold, ductility)
+    rate = each(lambda b: b * math.log2(math.e), brittleness)
 
     def step(x, carry):
+        lab = labels[x]
         moved = pltpu.roll(second_last[...], 127 - x, 1)
         end = jnp.where(lane == 127, moved, second[x, :, 128:256])
         whole = jnp.concatenate([second[x, :, 0:128], end], axis=1)
-        stress[x] = pick(labels[x], table, 3) * jnp.sqrt(whole)
+        stress[x] = pick(lab, stiff) * root(whole)
+        start[x] = pick(lab, threshold)
+        lost[x] = pick(lab, gone)
+        ductile[x] = pick(lab, ductility)
+        brittle[x] = pick(lab, rate)
         return carry
 
-    lax.fori_loop(0, 32, step, 0, unroll=2)
-
-
-def finish_cells(table, lab, averaged, history, stress):
+    lax.fori_loop(0, 32, step, 0, unroll=4)
+
+
+def finish_cells(averaged, history, stress, start, lost, ductile, brittle):
     kappa = jnp.maximum(history, averaged)
-    start = pick(lab, table, 4)
-    grown = (
-        1.0
-        - pick(lab, table, 5) / jnp.maximum(kappa, start)
-        - pick(lab, table, 6) * jnp.exp(pick(lab, table, 7) * (start - kappa))
-    )
+    grown = 1.0 - lost / kappa - ductile * jnp.exp2(brittle * (start - kappa))
     harm = jnp.where(kappa > start, grown, 0.0)
     return harm, (1.0 - harm) * stress
 
 
-def finish_planes(
-    table, window, count, first, inverse, history, stress, labels, d_buf, m_buf, damage, mises, sem
-):
+def finish_planes(window, count, first, inverse, fields, d_buf, m_buf, damage, mises, sem):
     g = taps()
 
     def step(k):
@@ -454,9 +458,7 @@
             for s in range(1, 9):
                 total = total + g[8 + s] * (cells[i + 8 - s] + cells[i + 8 + s])
             at = (first + i, rows, lanes)
-            harm, von_mises = finish_cells(
-                table, labels[at], total * inverse[at], history[at], stress[at]
-            )
+            harm, von_mises = finish_cells(total * inverse[at], *(f[at] for f in fields))
             d_buf[i, rows, lanes] = harm
             m_buf[i, rows, lanes] = von_mises
 
@@ -482,9 +484,7 @@
             copy.wait()
 
 
-def finish_most_kernel(
-    table, odd, field, near, inverse, history, stress, labels, damage, mises, d_buf, m_buf, sem
-):
+def finish_most_kernel(odd, field, near, inverse, *refs):
     is_odd, shift = odd[0] == 1, 8 * odd[0]
 
     def window(w, rows, lanes):
@@ -495,15 +495,11 @@
         return jnp.where(is_odd, field[w - 8, rows, lanes], near[w - 32, rows, lanes])
 
     first = 8 - shift
-    finish_planes(
-        table, window, 24, first, inverse, history, stress, labels, d_buf, m_buf, damage, mises, sem
-    )
-
-
-def finish_rest_kernel(
-    table, odd, field, far, inverse, history, stress, labels, d_in, m_in, damage, mises, d_buf, m_buf, sem
-):
-    del d_in, m_in
+    damage, mises, d_buf, m_buf, sem = refs[6:]
+    finish_planes(window, 24, first, inverse, refs[:6], d_buf, m_buf, damage, mises, sem)
+
+
+def finish_rest_kernel(odd, field, far, inverse, *refs):
     is_odd, shift = odd[0] == 1, 8 * odd[0]
 
     def window(w, rows, lanes):
@@ -514,9 +510,8 @@
         return jnp.where(is_odd, far[w - 16, rows, lanes], field[w - 8, rows, lanes])
 
     first = 3 * shift
-    finish_planes(
-        table, window, 8, first, inverse, history, stress, labels, d_buf, m_buf, damage, mises, sem
-    )
+    damage, mises, d_buf, m_buf, sem = refs[8:]
+    finish_planes(window, 8, first, inverse, refs[:6], d_buf, m_buf, damage, mises, sem)
 
 
 def shards(
@@ -531,9 +526,6 @@
     brittleness,
     weight,
 ):
-    (table,) = call(
-        table_kernel, [(8, 4)], n_in=6, smem=range(6), out_spaces=[pltpu.SMEM], limit=1 << 20
-    )(modulus, poisson, threshold, ductility, brittleness, weight)
     gz = jnp.stack([jnp.asarray(m) for m in split_const(band(256, 256, 0).T)])
     low, high = band(256, 8, -8).T, band(256, 8, 256).T
     own = band(256, 256, 0).T[255:256]
@@ -544,56 +536,60 @@
 
     field3, edge_x, edge_y = (32, 32, 256), (8, 32, 256), (32, 8, 256)
     hbm, vmem, dma = pltpu.HBM, pltpu.VMEM, pltpu.SemaphoreType.DMA
-    xm, ym, displacement = call(
-        planes_kernel, [(3, 32, 256), (3, 32, 256), displacement.shape], scratch=[dma((1,))]
+    xm, ym, xym, displacement = call(
+        planes_kernel, [(3, 32, 256), (3, 32, 256), (8, 256), displacement.shape], scratch=[dma((1,))],
     )(displacement)
     x_token = xm
     xm = shift_route(xm, ("gx",), (-1,))
+    ym = shift_route(ym, ("gy",), (-1,))
+    xym = shift_route(xym, ("gx", "gy"), (-1, -1))
     near, far = call(
         weight_edges_kernel, [edge_x, edge_x], spaces=[None, hbm],
         scratch=[vmem(edge_x, jnp.int32), vmem(edge_x, jnp.int32), dma((2,))], smem=(0,), odd=1,
         after=(x_token,),
     )(weight, labels)
-    w_near, w_far = swap_route(near, "gx", 0), swap_route(far, "gx", 1)
-    (ym,) = call(extend_kernel, [(3, 40, 256)], n_in=2, after=(near,))(ym, xm)
-    y_token = ym
-    ym = shift_route(ym, ("gy",), (-1,))
-    (nodes,) = call(columns_kernel, [(96, 128)], n_in=2, after=(y_token,))(displacement, labels)
-    top, second = call(strain_kernel, [field3, field3], n_in=6, smem=(0, 1))(
-        table, applied_strain, displacement, xm, ym, labels
-    )
-    (mine,) = call(zpack_kernel, [(240, 128)], n_in=4)(top, nodes, xm, ym)
+    w_near = swap_route(near, "gx", 0)
+    w_far = swap_route(far, "gx", 1)
+    (nodes,) = call(columns_kernel, [(96, 128)], n_in=2, after=(near,))(displacement, labels)
+    top, second = call(strain_kernel, [field3, field3], n_in=8, smem=(0, 1, 2))(
+        weight, poisson, applied_strain, displacement, xm, ym, xym, labels
+    )
+    (mine,) = call(zpack_kernel, [(240, 128)], n_in=5)(top, nodes, xm, ym, xym)
     peer = shift_route(mine, ("gz",), (1,))
     weights, near, far = call(
         weights_x_kernel, [field3, edge_y, edge_y], n_in=4, smem=(0,), odd=1, after=(mine,)
-    )(table, labels, w_near, w_far)
+    )(weight, labels, w_near, w_far)
     w_near, w_far = swap_route(near, "gy", 0), swap_route(far, "gy", 1)
     (local,) = call(z_local_kernel, [field3], n_in=2, after=(near,))(top, gz)
     top, near, far, second_last = call(
-        top_z_kernel, [field3, edge_y, edge_y, (32, 128)], scratch=[vmem((32, 128), F32)], n_in=6, smem=(0, 1), odd=2
-    )(table, applied_strain, local, mine, peer, gh)
+        top_z_kernel, [field3, edge_y, edge_y, (32, 128)], scratch=[vmem((32, 128), F32)], n_in=7, smem=(0, 1, 2), odd=3
+    )(weight, poisson, applied_strain, local, mine, peer, gh)
     t_near, t_far = swap_route(near, "gy", 0), swap_route(far, "gy", 1)
+    phases = call(
+        phases_kernel, [field3] * 5, n_in=8, smem=range(5), after=(near,)
+    )(modulus, poisson, threshold, ductility, brittleness, labels, second, second_last)
     weights, cols = call(
-        weights_y_kernel, [field3, (128, 128)], n_in=5, odd=0, after=(near,)
+        weights_y_kernel, [field3, (128, 128)], n_in=5, odd=0, after=(phases[0],)
     )(weights, w_near, w_far, gy, gz)
     z_token = cols
     cols = shift_route(cols, ("gz",), (1,))
-    (stress,) = call(stress_kernel, [field3], n_in=4, smem=(0,), after=(z_token,))(table, labels, second, second_last)
-    top, near, far = call(top_y_kernel, [field3, edge_x, edge_x], n_in=4, odd=0, after=(stress,))(
-        top, t_near, t_far, gy
-    )
+    top, near, far = call(
+        top_y_kernel, [field3, edge_x, edge_x], n_in=4, odd=0, after=(z_token,)
+    )(top, t_near, t_far, gy)
     (inverse,) = call(weights_z_kernel, [field3], n_in=3, after=(near,))(weights, cols, gh)
-    near, far = swap_route(near, "gx", 0), swap_route(far, "gx", 1)
+    far = swap_route(far, "gx", 1)
+    near = swap_route(near, "gx", 0)
     outs = [field3, field3]
+    fields = (inverse, history, *phases)
     damage, mises = call(
-        finish_most_kernel, outs, n_in=7, smem=(0,), odd=1, out_spaces=[hbm, hbm],
+        finish_most_kernel, outs, n_in=9, odd=0, out_spaces=[hbm, hbm],
         scratch=[vmem((24, 32, 256), F32), vmem((24, 32, 256), F32), dma((2, 4))],
-    )(table, top, near, inverse, history, stress, labels)
+    )(top, near, *fields)
     return call(
-        finish_rest_kernel, outs, smem=(0,), odd=1, out_spaces=[hbm, hbm],
-        spaces=[None] * 7 + [hbm, hbm], aliases={7: 0, 8: 1},
+        finish_rest_kernel, outs, odd=0, out_spaces=[hbm, hbm],
+        spaces=[None] * 9 + [hbm, hbm], aliases={9: 0, 10: 1},
         scratch=[vmem((8, 32, 256), F32), vmem((8, 32, 256), F32), dma((2, 4))],
-    )(table, top, far, inverse, history, stress, labels, damage, mises)
+    )(top, far, *fields, damage, mises)
 
 
 def solution(mesh):

time: 69.9 us -> 67.3 us (0.963)
  Pallas kernels: 24.6 us -> 20 us
  starting transfers between devices: 26.4 us -> 28.6 us
    pallas_call x16 -> x14, Pallas kernels: 24.6 us -> 20 us  [call(): return lambda *args: built(*args, *after)]
    ppermute x4 -> x5, waiting for transfers between devices: 9.17 us -> 10.6 us  [shift_route(): return lax.ppermute(block, axes if len(axes) > 1 else axes[0], route)]
    ppermute x4 -> x5, starting transfers between devices: 15.3 us -> 16.6 us  [shift_route(): return lax.ppermute(block, axes if len(axes) > 1 else axes[0], route)]
    ppermute x8, waiting for transfers between devices: 5.55 us -> 4.46 us  [swap_route(): return lax.ppermute(block, axis, route)]
    ppermute x8, starting transfers between devices: 11.1 us -> 12 us  [swap_route(): return lax.ppermute(block, axis, route)]
  transfers between devices with their start and end apart: 12 -> 13, of which waited for: 4 -> 5; matrix products, arithmetic and copies ran while one was open for 0% -> 0% of each run, Pallas kernels for 31% -> 25%
where the time goes in v1:
time: 67.3 us; the launch traced here: 66.9 us
  starting transfers between devices  28.6 us (42%)
  Pallas kernels  20 us (30%)
  waiting for transfers between devices  15 us (22%)
  local copies, waits for them, and re-layouts  2.44 us (4%)
  between operations  0.9 us (1%)
    pallas_call x14, Pallas kernels, call(): return lambda *args: built(*args, *after)  20 us
    ppermute x5, starting transfers between devices, shift_route(): return lax.ppermute(block, axes if len(axes) > 1 else axes[0], route)  16.6 us
    ppermute x8, starting transfers between devices, swap_route(): return lax.ppermute(block, axis, route)  12 us
    ppermute x5, waiting for transfers between devices, shift_route(): return lax.ppermute(block, axes if len(axes) > 1 else axes[0], route)  10.6 us
    ppermute x8, waiting for transfers between devices, swap_route(): return lax.ppermute(block, axis, route)  4.46 us
    unnamed x26, local copies, waits for them, and re-layouts  2.44 us
  transfers between devices with their start and end apart: 13, of which 5 were waited for; matrix products, arithmetic and copies ran while one was open for 0% of the time, Pallas kernels for 25%

profile of v1, /device:TPU:32, one launch (start us, length us, event | category | flops | bytes accessed | tf_op | source)
XLA Modules:
  0.0 66.9 jit_solution(14254932791929508826)
XLA Ops:
  0.6 0.0 copy-start
  0.6 0.0 copy-start.2
  0.6 2.0 %copy-done.2 = f32[3,32,32,256]{3,2,1,0:T(8,128)S(1)} copy-done((f32[3,32,32,256]{3,2,1,0:T(8,128)S(1)}, f32[3,32,32,256]{3,2,1,0:T(8,128)}, u32[]{:S(2)}) %copy-start.2) | copy-done | bytes 3145752
  2.6 0.3 shard_map.149
  2.9 0.0 copy-start.7
  2.9 0.0 copy-start.8
  2.9 0.0 copy-done
  2.9 0.4 copy-done.6
  3.3 0.7 %shard_map.151 = (f32[8,32,256]{2,1,0:T(8,128)S(1)}, f32[8,32,256]{2,1,0:T(8,128)S(1)}) custom-call(f32[4]{0:T(128)S(1)} %copy-done.6, s32[32,32,256]{2,1,0:T(8,128)S(1)} %copy-done, f32[3,32,256]{2,1,0:T(8,128)S(1)} %get-tuple-element.30.refs_2_), custom_call_target="tpu_custom_call" | custom-call | tf_op jit(solution)/shard_map/pallas_call | solution.py:94
  4.1 0.1 collective-permute-start.4
  4.2 2.0 %collective-permute-start.3 = (f32[8,32,256]{2,1,0:T(8,128)S(1)}, f32[8,32,256]{2,1,0:T(8,128)S(1)}, u32[]{:S(2)}, u32[]{:S(2)}) collective-permute-start(f32[8,32,256]{2,1,0:T(8,128)S(1)} %get-tuple-element.34.refs_2_), channel_id=1, source_target_pairs={{0,32},{32,0},{64,96},{96,64},{128,160},{160,128},{192,224},{224,1... | collective-permute-start | bytes 786440 | tf_op jit(solution)/shard_map/ppermute | solution.py:65
  6.2 5.2 %collective-permute-start.1 = (f32[3,32,256]{2,1,0:T(8,128)S(1)}, f32[3,32,256]{2,1,0:T(8,128)S(1)}, u32[]{:S(2)}, u32[]{:S(2)}) collective-permute-start(f32[3,32,256]{2,1,0:T(8,128)S(1)} %get-tuple-element.31), channel_id=1, source_target_pairs={{0,30},{2,0},{4,2},{6,4},{8,6},{10,8},{12,10},{14,12},{16,14},{18,... | collective-permute-start | bytes 294920 | tf_op jit(solution)/shard_map/ppermute | solution.py:56
  11.4 2.0 %collective-permute-start = (f32[3,32,256]{2,1,0:T(8,128)S(1)}, f32[3,32,256]{2,1,0:T(8,128)S(1)}, u32[]{:S(2)}, u32[]{:S(2)}) collective-permute-start(f32[3,32,256]{2,1,0:T(8,128)S(1)} %get-tuple-element.30.refs_2_), channel_id=1, source_target_pairs={{0,224},{32,0},{64,32},{96,64},{128,96},{160,128},{192,160},{224,1... | collective-permute-start | bytes 294920 | tf_op jit(solution)/shard_map/ppermute | solution.py:56
  13.4 0.5 collective-permute-start.2
  13.8 1.2 %shard_map.152.refs_1_ = f32[96,128]{1,0:T(8,128)S(1)} custom-call(f32[3,32,32,256]{3,2,1,0:T(8,128)S(1)} %get-tuple-element.29.refs_3_.refs_0_, s32[32,32,256]{2,1,0:T(8,128)S(1)} %copy-done, f32[8,32,256]{2,1,0:T(8,128)S(1)} %get-tuple-element.34.refs_2_), custom_call_target="tpu_custom_call" | custom-call | tf_op jit(solution)/shard_map/pallas_call | solution.py:94
  15.1 0.0 copy-start.3
  15.1 1.4 %collective-permute-done.2.refs_6_.refs_4_ = f32[8,256]{1,0:T(8,128)S(1)} collective-permute-done((f32[8,256]{1,0:T(8,128)S(1)}, f32[8,256]{1,0:T(8,128)S(1)}, u32[]{:S(2)}, u32[]{:S(2)}) %collective-permute-start.2) | collective-permute-done | bytes 8224 | tf_op jit(solution)/shard_map/ppermute | solution.py:56
  16.5 0.0 collective-permute-done.1.refs_5_.refs_3_
  16.5 0.0 collective-permute-done.refs_4_.refs_2_
  16.5 0.0 copy-done.7
  16.5 0.0 copy-done.8
  16.5 5.3 %shard_map.150 = (f32[32,32,256]{2,1,0:T(8,128)S(1)}, f32[32,32,256]{2,1,0:T(8,128)S(1)}) custom-call(f32[4]{0:T(128)S(1)} %copy-done.6, f32[4]{0:T(128)S(1)} %copy-done.7, f32[6]{0:T(128)S(1)} %copy-done.8, f32[3,32,32,256]{3,2,1,0:T(8,128)S(1)} %get-tuple-element.29.refs_3_.refs_0_, f32[3,32,256]{2,1,0:T(8,128)S(1)} %collective-permute-done.refs_4_.refs_2_, ...), custom_call_target="tpu_custom_call" | custom-call | tf_op jit(solution)/shard_map/pallas_call | solution.py:94
  21.8 0.0 copy-start.4
  21.8 0.6 shard_map.153.refs_4_
  22.4 0.0 copy-start.9
  22.4 0.0 copy-start.10
  22.4 0.0 copy-start.11
  22.4 0.0 copy-start.12
  22.5 4.6 %collective-permute-start.5 = (f32[240,128]{1,0:T(8,128)S(1)}, f32[240,128]{1,0:T(8,128)S(1)}, u32[]{:S(2)}, u32[]{:S(2)}) collective-permute-start(f32[240,128]{1,0:T(8,128)S(1)} %shard_map.153.refs_4_), channel_id=1, source_target_pairs={{0,1},{1,0},{2,3},{3,2},{4,5},{5,4},{6,7},{7,6},{8,9},{9,8},{10,11... | collective-permute-start | bytes 368648 | tf_op jit(solution)/shard_map/ppermute | solution.py:56
  27.0 0.0 collective-permute-done.4.refs_3_
  27.0 0.0 collective-permute-done.3.refs_2_
  27.0 1.8 %shard_map.154 = (f32[32,32,256]{2,1,0:T(8,128)S(1)}, f32[32,8,256]{2,1,0:T(8,128)S(1)}, f32[32,8,256]{2,1,0:T(8,128)S(1)}) custom-call(f32[4]{0:T(128)S(1)} %copy-done.6, s32[32,32,256]{2,1,0:T(8,128)S(1)} %copy-done, f32[8,32,256]{2,1,0:T(8,128)S(1)} %collective-permute-done.3.refs_2_, f32[8,32,256]{2,1,0:T(8,128)S(1)} %collective-permute-done.4.refs_3_, ...), custom_call_target="tpu_custom_call" | custom-call | tf_op jit(solution)/shard_map/pallas_call | solution.py:94
  28.9 0.0 copy-start.5
  28.9 0.1 collective-permute-start.8
  29.0 0.0 copy-done.3
  29.0 0.6 shard_map.155.refs_3_
  29.6 4.1 %collective-permute-start.9 = (f32[32,8,256]{2,1,0:T(8,128)S(1)}, f32[32,8,256]{2,1,0:T(8,128)S(1)}, u32[]{:S(2)}, u32[]{:S(2)}) collective-permute-start(f32[32,8,256]{2,1,0:T(8,128)S(1)} %get-tuple-element.41), channel_id=1, source_target_pairs={{2,4},{4,2},{6,8},{8,6},{10,12},{12,10},{14,16},{16,14},{18,20},{2... | collective-permute-start | bytes 786440 | tf_op jit(solution)/shard_map/ppermute | solution.py:65
  33.7 0.4 collective-permute-done.5.refs_5_
  34.1 0.0 copy-done.4
  34.1 1.5 %shard_map.156 = (f32[32,32,256]{2,1,0:T(8,128)S(1)}, f32[32,8,256]{2,1,0:T(8,128)S(1)}, f32[32,8,256]{2,1,0:T(8,128)S(1)}, f32[32,128]{1,0:T(8,128)S(1)}) custom-call(f32[4]{0:T(128)S(1)} %copy-done.6, f32[4]{0:T(128)S(1)} %copy-done.7, f32[6]{0:T(128)S(1)} %copy-done.8, f32[32,32,256]{2,1,0:T(8,128)S(1)} %shard_map.155.refs_3_, ...), custom_call_target="tpu_custom_call" | custom-call | tf_op jit(solution)/shard_map/pallas_call | solution.py:94
  35.6 4.6 %collective-permute-start.7 = (f32[32,8,256]{2,1,0:T(8,128)S(1)}, f32[32,8,256]{2,1,0:T(8,128)S(1)}, u32[]{:S(2)}, u32[]{:S(2)}) collective-permute-start(f32[32,8,256]{2,1,0:T(8,128)S(1)} %get-tuple-element.39), channel_id=1, source_target_pairs={{2,4},{4,2},{6,8},{8,6},{10,12},{12,10},{14,16},{16,14},{18,20},{2... | collective-permute-start | bytes 786440 | tf_op jit(solution)/shard_map/ppermute | solution.py:65
  40.2 0.0 collective-permute-start.6
  40.2 0.0 copy-done.9
  40.2 0.0 copy-done.10
  40.2 0.0 copy-done.11
  40.2 0.0 copy-done.12
  40.2 1.5 %shard_map.157 = (f32[32,32,256]{2,1,0:T(8,128)S(1)}, f32[32,32,256]{2,1,0:T(8,128)S(1)}, f32[32,32,256]{2,1,0:T(8,128)S(1)}, f32[32,32,256]{2,1,0:T(8,128)S(1)}, f32[32,32,256]{2,1,0:T(8,128)S(1)}) custom-call(f32[4]{0:T(128)S(1)} %copy-done.9, f32[4]{0:T(128)S(1)} %copy-done.7, f32[4]{0:T(128)S(1)} %copy-done.10, f32[4]{0:T(128)S(1)} %copy-done.11, ...), custom_call_target="tpu_custom_call" | custom-call | tf_op jit(solution)/shard_map/pallas_call | solution.py:94
  41.7 0.4 collective-permute-done.9.refs_2_
  42.2 0.0 collective-permute-done.8.refs_1_
  42.2 0.0 copy-done.5
  42.2 1.5 %shard_map.158 = (f32[32,32,256]{2,1,0:T(8,128)S(1)}, f32[128,128]{1,0:T(8,128)S(1)}) custom-call(f32[32,32,256]{2,1,0:T(8,128)S(1)} %get-tuple-element.40.refs_0_, f32[32,8,256]{2,1,0:T(8,128)S(1)} %collective-permute-done.8.refs_1_, f32[32,8,256]{2,1,0:T(8,128)S(1)} %collective-permute-done.9.refs_2_, bf16[32,144]{1,0:T(8,128)(2,1)S(1)} %copy-done.5, ...), custom_call_target="tpu_custom_call" | custom-call | tf_op jit(solution)/shard_map/pallas_call | solution.py:94
  43.7 4.0 %collective-permute-done.7.refs_2_ = f32[32,8,256]{2,1,0:T(8,128)S(1)} collective-permute-done((f32[32,8,256]{2,1,0:T(8,128)S(1)}, f32[32,8,256]{2,1,0:T(8,128)S(1)}, u32[]{:S(2)}, u32[]{:S(2)}) %collective-permute-start.7) | collective-permute-done | bytes 262176 | tf_op jit(solution)/shard_map/ppermute | solution.py:65
  47.7 0.0 collective-permute-done.6.refs_1_
  47.7 0.9 %shard_map.159 = (f32[32,32,256]{2,1,0:T(8,128)S(1)}, f32[8,32,256]{2,1,0:T(8,128)S(1)}, f32[8,32,256]{2,1,0:T(8,128)S(1)}) custom-call(f32[32,32,256]{2,1,0:T(8,128)S(1)} %get-tuple-element.37.refs_0_, f32[32,8,256]{2,1,0:T(8,128)S(1)} %collective-permute-done.6.refs_1_, f32[32,8,256]{2,1,0:T(8,128)S(1)} %collective-permute-done.7.refs_2_, ...), custom_call_target="tpu_custom_call" | custom-call | tf_op jit(solution)/shard_map/pallas_call | solution.py:94
  48.6 0.1 collective-permute-start.12
  48.7 1.0 %collective-permute-start.10 = (f32[8,32,256]{2,1,0:T(8,128)S(1)}, f32[8,32,256]{2,1,0:T(8,128)S(1)}, u32[]{:S(2)}, u32[]{:S(2)}) collective-permute-start(f32[8,32,256]{2,1,0:T(8,128)S(1)} %get-tuple-element.47), channel_id=1, source_target_pairs={{32,64},{64,32},{96,128},{128,96},{160,192},{192,160},{224,0},{0,2... | collective-permute-start | bytes 786440 | tf_op jit(solution)/shard_map/ppermute | solution.py:65
  49.8 4.3 %collective-permute-start.11 = (f32[128,128]{1,0:T(8,128)S(1)}, f32[128,128]{1,0:T(8,128)S(1)}, u32[]{:S(2)}, u32[]{:S(2)}) collective-permute-start(f32[128,128]{1,0:T(8,128)S(1)} %get-tuple-element.45.refs_4_), channel_id=1, source_target_pairs={{0,1},{1,0},{2,3},{3,2},{4,5},{5,4},{6,7},{7,6},{8,9},{9,8},{10,11... | collective-permute-start | bytes 196616 | tf_op jit(solution)/shard_map/ppermute | solution.py:56
  54.1 8.8 %collective-permute-done.11.refs_1_ = f32[128,128]{1,0:T(8,128)S(1)} collective-permute-done((f32[128,128]{1,0:T(8,128)S(1)}, f32[128,128]{1,0:T(8,128)S(1)}, u32[]{:S(2)}, u32[]{:S(2)}) %collective-permute-start.11) | collective-permute-done | bytes 65568 | tf_op jit(solution)/shard_map/ppermute | solution.py:56
  62.9 0.6 shard_map.160.refs_2_
  63.5 0.0 collective-permute-done.12.refs_1_
  63.5 0.0 copy-done.1
  63.5 2.1 %shard_map.161 = (f32[32,32,256]{2,1,0:T(8,128)}, f32[32,32,256]{2,1,0:T(8,128)}) custom-call(f32[32,32,256]{2,1,0:T(8,128)S(1)} %get-tuple-element.46.refs_0_, f32[8,32,256]{2,1,0:T(8,128)S(1)} %collective-permute-done.12.refs_1_, f32[32,32,256]{2,1,0:T(8,128)S(1)} %shard_map.160.refs_2_, f32[32,32,256]{2,1,0:T(8,128)S(1)} %copy-done.1, ...), custom_call_target="tpu_custom_call" | custom-call | tf_op jit(solution)/shard_map/pallas_call | solution.py:94
  65.6 0.0 collective-permute-done.10.refs_1_
  65.6 1.3 %shard_map.162 = (f32[32,32,256]{2,1,0:T(8,128)}, f32[32,32,256]{2,1,0:T(8,128)}) custom-call(f32[32,32,256]{2,1,0:T(8,128)S(1)} %get-tuple-element.46.refs_0_, f32[8,32,256]{2,1,0:T(8,128)S(1)} %collective-permute-done.10.refs_1_, f32[32,32,256]{2,1,0:T(8,128)S(1)} %shard_map.160.refs_2_, ...), custom_call_target="tpu_custom_call", output_to_operand_aliasing={{0}: (9, {}), {1}: (10, {})} | custom-call | tf_op jit(solution)/shard_map/pallas_call | solution.py:94
  (2 shorter events, 0.0 us)
Async XLA Ops:
  0.6 2.3 %copy-start = (s32[32,32,256]{2,1,0:T(8,128)S(1)}, s32[32,32,256]{2,1,0:T(8,128)}, u32[]{:S(2)}) copy-start(s32[32,32,256]{2,1,0:T(8,128)} %refs_5_.1) | copy-start | bytes 3145732
  0.6 2.0 %copy-start.2 = (f32[3,32,32,256]{3,2,1,0:T(8,128)S(1)}, f32[3,32,32,256]{3,2,1,0:T(8,128)}, u32[]{:S(2)}) copy-start(f32[3,32,32,256]{3,2,1,0:T(8,128)} %refs_0_.6) | copy-start | bytes 9437188
  2.6 0.7 %copy-start.6 = (f32[4]{0:T(128)S(1)}, f32[4]{0:T(128)}, u32[]{:S(2)}) copy-start(f32[4]{0:T(128)} %refs_0_.10) | copy-start | bytes 52
  2.9 13.6 %copy-start.7 = (f32[4]{0:T(128)S(1)}, f32[4]{0:T(128)}, u32[]{:S(2)}) copy-start(f32[4]{0:T(128)} %refs_1_.11) | copy-start | bytes 52
  2.9 13.6 %copy-start.8 = (f32[6]{0:T(128)S(1)}, f32[6]{0:T(128)}, u32[]{:S(2)}) copy-start(f32[6]{0:T(128)} %refs_2_.5) | copy-start | bytes 76
  4.1 23.0 %collective-permute-start.4 = (f32[8,32,256]{2,1,0:T(8,128)S(1)}, f32[8,32,256]{2,1,0:T(8,128)S(1)}, u32[]{:S(2)}, u32[]{:S(2)}) collective-permute-start(f32[8,32,256]{2,1,0:T(8,128)S(1)} %get-tuple-element.35), channel_id=1, source_target_pairs={{32,64},{64,32},{96,128},{128,96},{160,192},{192,160},{224,0},{0,2... | collective-permute-start | bytes 786440 | tf_op jit(solution)/shard_map/ppermute | solution.py:65
  4.2 22.9 %collective-permute-start.3 = (f32[8,32,256]{2,1,0:T(8,128)S(1)}, f32[8,32,256]{2,1,0:T(8,128)S(1)}, u32[]{:S(2)}, u32[]{:S(2)}) collective-permute-start(f32[8,32,256]{2,1,0:T(8,128)S(1)} %get-tuple-element.34.refs_2_), channel_id=1, source_target_pairs={{0,32},{32,0},{64,96},{96,64},{128,160},{160,128},{192,224},{224,1... | collective-permute-start | bytes 786440 | tf_op jit(solution)/shard_map/ppermute | solution.py:65
  6.2 10.3 %collective-permute-start.1 = (f32[3,32,256]{2,1,0:T(8,128)S(1)}, f32[3,32,256]{2,1,0:T(8,128)S(1)}, u32[]{:S(2)}, u32[]{:S(2)}) collective-permute-start(f32[3,32,256]{2,1,0:T(8,128)S(1)} %get-tuple-element.31), channel_id=1, source_target_pairs={{0,30},{2,0},{4,2},{6,4},{8,6},{10,8},{12,10},{14,12},{16,14},{18,... | collective-permute-start | bytes 294920 | tf_op jit(solution)/shard_map/ppermute | solution.py:56
  11.4 5.1 %collective-permute-start = (f32[3,32,256]{2,1,0:T(8,128)S(1)}, f32[3,32,256]{2,1,0:T(8,128)S(1)}, u32[]{:S(2)}, u32[]{:S(2)}) collective-permute-start(f32[3,32,256]{2,1,0:T(8,128)S(1)} %get-tuple-element.30.refs_2_), channel_id=1, source_target_pairs={{0,224},{32,0},{64,32},{96,64},{128,96},{160,128},{192,160},{224,1... | collective-permute-start | bytes 294920 | tf_op jit(solution)/shard_map/ppermute | solution.py:56
  13.4 3.1 %collective-permute-start.2 = (f32[8,256]{1,0:T(8,128)S(1)}, f32[8,256]{1,0:T(8,128)S(1)}, u32[]{:S(2)}, u32[]{:S(2)}) collective-permute-start(f32[8,256]{1,0:T(8,128)S(1)} %get-tuple-element.32), channel_id=1, source_target_pairs={{0,254},{2,224},{4,226},{6,228},{8,230},{10,232},{12,234},{14,236}... | collective-permute-start | bytes 24584 | tf_op jit(solution)/shard_map/ppermute | solution.py:56
  15.1 13.9 %copy-start.3 = (bf16[2,256,256]{2,1,0:T(8,128)(2,1)S(1)}, bf16[2,256,256]{2,1,0:T(8,128)(2,1)}, u32[]{:S(2)}) copy-start(bf16[2,256,256]{2,1,0:T(8,128)(2,1)} %constant.14.refs_1_.refs_4_) | copy-start | bytes 786436
  21.8 12.3 %copy-start.4 = (bf16[72,256]{1,0:T(8,128)(2,1)S(1)}, bf16[72,256]{1,0:T(8,128)(2,1)}, u32[]{:S(2)}) copy-start(bf16[72,256]{1,0:T(8,128)(2,1)} %constant.10.clone.refs_6_.refs_2_) | copy-start | bytes 110596
  22.4 17.8 %copy-start.9 = (f32[4]{0:T(128)S(1)}, f32[4]{0:T(128)}, u32[]{:S(2)}) copy-start(f32[4]{0:T(128)} %refs_0_.11) | copy-start | bytes 52
  22.4 17.8 %copy-start.10 = (f32[4]{0:T(128)S(1)}, f32[4]{0:T(128)}, u32[]{:S(2)}) copy-start(f32[4]{0:T(128)} %refs_2_.6) | copy-start | bytes 52
  22.4 17.8 %copy-start.11 = (f32[4]{0:T(128)S(1)}, f32[4]{0:T(128)}, u32[]{:S(2)}) copy-start(f32[4]{0:T(128)} %refs_3_.5) | copy-start | bytes 52
  22.4 17.8 %copy-start.12 = (f32[4]{0:T(128)S(1)}, f32[4]{0:T(128)}, u32[]{:S(2)}) copy-start(f32[4]{0:T(128)} %refs_4_.1) | copy-start | bytes 52
  22.5 11.7 %collective-permute-start.5 = (f32[240,128]{1,0:T(8,128)S(1)}, f32[240,128]{1,0:T(8,128)S(1)}, u32[]{:S(2)}, u32[]{:S(2)}) collective-permute-start(f32[240,128]{1,0:T(8,128)S(1)} %shard_map.153.refs_4_), channel_id=1, source_target_pairs={{0,1},{1,0},{2,3},{3,2},{4,5},{5,4},{6,7},{7,6},{8,9},{9,8},{10,11... | collective-permute-start | bytes 368648 | tf_op jit(solution)/shard_map/ppermute | solution.py:56
  28.9 13.3 %copy-start.5 = (bf16[32,144]{1,0:T(8,128)(2,1)S(1)}, bf16[32,144]{1,0:T(8,128)(2,1)}, u32[]{:S(2)}) copy-start(bf16[32,144]{1,0:T(8,128)(2,1)} %constant.11.clone.refs_3_) | copy-start | bytes 27652
  28.9 13.3 %collective-permute-start.8 = (f32[32,8,256]{2,1,0:T(8,128)S(1)}, f32[32,8,256]{2,1,0:T(8,128)S(1)}, u32[]{:S(2)}, u32[]{:S(2)}) collective-permute-start(f32[32,8,256]{2,1,0:T(8,128)S(1)} %get-tuple-element.36.refs_2_), channel_id=1, source_target_pairs={{0,2},{2,0},{4,6},{6,4},{8,10},{10,8},{12,14},{14,12},{16,18},{18,... | collective-permute-start | bytes 786440 | tf_op jit(solution)/shard_map/ppermute | solution.py:65
  29.6 12.6 %collective-permute-start.9 = (f32[32,8,256]{2,1,0:T(8,128)S(1)}, f32[32,8,256]{2,1,0:T(8,128)S(1)}, u32[]{:S(2)}, u32[]{:S(2)}) collective-permute-start(f32[32,8,256]{2,1,0:T(8,128)S(1)} %get-tuple-element.41), channel_id=1, source_target_pairs={{2,4},{4,2},{6,8},{8,6},{10,12},{12,10},{14,16},{16,14},{18,20},{2... | collective-permute-start | bytes 786440 | tf_op jit(solution)/shard_map/ppermute | solution.py:65
  35.6 12.1 %collective-permute-start.7 = (f32[32,8,256]{2,1,0:T(8,128)S(1)}, f32[32,8,256]{2,1,0:T(8,128)S(1)}, u32[]{:S(2)}, u32[]{:S(2)}) collective-permute-start(f32[32,8,256]{2,1,0:T(8,128)S(1)} %get-tuple-element.39), channel_id=1, source_target_pairs={{2,4},{4,2},{6,8},{8,6},{10,12},{12,10},{14,16},{16,14},{18,20},{2... | collective-permute-start | bytes 786440 | tf_op jit(solution)/shard_map/ppermute | solution.py:65
  40.2 7.5 %collective-permute-start.6 = (f32[32,8,256]{2,1,0:T(8,128)S(1)}, f32[32,8,256]{2,1,0:T(8,128)S(1)}, u32[]{:S(2)}, u32[]{:S(2)}) collective-permute-start(f32[32,8,256]{2,1,0:T(8,128)S(1)} %get-tuple-element.38.refs_8_), channel_id=1, source_target_pairs={{0,2},{2,0},{4,6},{6,4},{8,10},{10,8},{12,14},{14,12},{16,18},{18,... | collective-permute-start | bytes 786440 | tf_op jit(solution)/shard_map/ppermute | solution.py:65
  42.2 21.3 %copy-start.1 = (f32[32,32,256]{2,1,0:T(8,128)S(1)}, f32[32,32,256]{2,1,0:T(8,128)}, u32[]{:S(2)}) copy-start(f32[32,32,256]{2,1,0:T(8,128)} %refs_3_.7) | copy-start | bytes 3145732
  48.6 14.8 %collective-permute-start.12 = (f32[8,32,256]{2,1,0:T(8,128)S(1)}, f32[8,32,256]{2,1,0:T(8,128)S(1)}, u32[]{:S(2)}, u32[]{:S(2)}) collective-permute-start(f32[8,32,256]{2,1,0:T(8,128)S(1)} %get-tuple-element.49.refs_3_), channel_id=1, source_target_pairs={{0,32},{32,0},{64,96},{96,64},{128,160},{160,128},{192,224},{224,1... | collective-permute-start | bytes 786440 | tf_op jit(solution)/shard_map/ppermute | solution.py:65
  48.7 16.8 %collective-permute-start.10 = (f32[8,32,256]{2,1,0:T(8,128)S(1)}, f32[8,32,256]{2,1,0:T(8,128)S(1)}, u32[]{:S(2)}, u32[]{:S(2)}) collective-permute-start(f32[8,32,256]{2,1,0:T(8,128)S(1)} %get-tuple-element.47), channel_id=1, source_target_pairs={{32,64},{64,32},{96,128},{128,96},{160,192},{192,160},{224,0},{0,2... | collective-permute-start | bytes 786440 | tf_op jit(solution)/shard_map/ppermute | solution.py:65
  49.8 13.1 %collective-permute-start.11 = (f32[128,128]{1,0:T(8,128)S(1)}, f32[128,128]{1,0:T(8,128)S(1)}, u32[]{:S(2)}, u32[]{:S(2)}) collective-permute-start(f32[128,128]{1,0:T(8,128)S(1)} %get-tuple-element.45.refs_4_), channel_id=1, source_target_pairs={{0,1},{1,0},{2,3},{3,2},{4,5},{5,4},{6,7},{7,6},{8,9},{9,8},{10,11... | collective-permute-start | bytes 196616 | tf_op jit(solution)/shard_map/ppermute | solution.py:56

commit v2 on v1

--- a/solution.py
+++ b/solution.py
@@ -120,24 +120,15 @@
     keep.wait()
 
 
-def weight_edges_kernel(weight, odd, labels, near, far, low, high, sem):
-    copies = [
-        pltpu.make_async_copy(labels.at[pl.ds(0, 8)], low, sem.at[0]),
-        pltpu.make_async_copy(labels.at[pl.ds(24, 8)], high, sem.at[1]),
-    ]
-    for copy in copies:
-        copy.start()
-    for copy in copies:
-        copy.wait()
-    is_odd = odd[0] == 1
+def weight_edges_kernel(weight, odd, labels, near, far):
+    start = 24 * (1 - odd[0])
 
     def step(i, carry):
-        a, b = pick(low[i], weight), pick(high[i], weight)
-        near[i] = jnp.where(is_odd, a, b)
-        far[i] = jnp.where(is_odd, b, a)
+        near[i] = pick(labels[start + i], weight)
+        far[i] = pick(labels[24 - start + i], weight)
         return carry
 
-    lax.fori_loop(0, 8, step, 0, unroll=2)
+    lax.fori_loop(0, 8, step, 0, unroll=8)
 
 
 def columns_kernel(u, labels, nodes):
@@ -177,15 +168,15 @@
 def response(poisson, weight):
     lead = each(lambda nu, w: 0.1125 * w / (1.0 - 2.0 * nu), poisson, weight)
     shear = each(lambda nu, w: w / (1.0 + nu), poisson, weight)
-    return lead, [(0.3 / 96.0) * (f * f) for f in shear]
+    return lead, [(0.3 / 48.0) * (f * f) for f in shear]
 
 
 def respond(applied, law, lab, sums):
     xx, yy, zz = (4.0 * applied[i] + sums[i] for i in range(3))
     xy, yz, xz = (8.0 * applied[i] + sums[j] for i, j in ((5, 3), (3, 4), (4, 5)))
     trace = xx + yy + zz
-    p, q, r = xx - yy, yy - zz, zz - xx
-    second = (p * p + q * q + r * r) + 1.5 * (yz * yz + xz * xz + xy * xy)
+    p, q = xx - yy, yy - zz
+    second = (p * (p + q) + q * q) + 0.75 * (yz * yz + xz * xz + xy * xy)
     lead = pick(lab, law[0]) * trace
     return lead + root(lead * lead + pick(lab, law[1]) * second), second
 
@@ -408,11 +399,26 @@
     z_local_kernel(out, gz, out)
 
 
-def top_y_kernel(odd, field, r_near, r_far, gy, out, near, far):
-    smooth_all_y(odd, field, r_near, r_far, gy, out)
-    start = 24 * (1 - odd[0])
-    near[...] = out[pl.ds(start, 8)]
-    far[...] = out[pl.ds(24 - start, 8)]
+def top_y_far_kernel(odd, field, r_near, r_far, gy, far):
+    is_odd, first = odd[1] == 1, 24 * odd[0]
+
+    def step(i, carry):
+        far[i] = smooth_y(first + i, is_odd, field, r_near, r_far, gy)
+        return carry
+
+    lax.fori_loop(0, 8, step, 0, unroll=8)
+
+
+def top_y_kernel(odd, field, r_near, r_far, gy, far, out, near):
+    is_odd, first = odd[1] == 1, 8 * (1 - odd[0])
+
+    def step(i, carry):
+        out[first + i] = smooth_y(first + i, is_odd, field, r_near, r_far, gy)
+        return carry
+
+    lax.fori_loop(0, 24, step, 0, unroll=8)
+    out[pl.ds(24 * odd[0], 8)] = far[...]
+    near[...] = out[pl.ds(24 * (1 - odd[0]), 8)]
 
 
 def phases_kernel(
@@ -420,7 +426,7 @@
     labels, second, second_last, stress, start, lost, ductile, brittle,
 ):
     lane = lax.broadcasted_iota(jnp.int32, (32, 128), 1)
-    stiff = each(lambda e, nu: math.sqrt(3.0 / 96.0) * e / (1.0 + nu), modulus, poisson)
+    stiff = each(lambda e, nu: math.sqrt(3.0 / 48.0) * e / (1.0 + nu), modulus, poisson)
     gone = each(lambda k, a: k * (1.0 - a), threshold, ductility)
     rate = each(lambda b: b * math.log2(math.e), brittleness)
 
@@ -543,14 +549,10 @@
     xm = shift_route(xm, ("gx",), (-1,))
     ym = shift_route(ym, ("gy",), (-1,))
     xym = shift_route(xym, ("gx", "gy"), (-1, -1))
-    near, far = call(
-        weight_edges_kernel, [edge_x, edge_x], spaces=[None, hbm],
-        scratch=[vmem(edge_x, jnp.int32), vmem(edge_x, jnp.int32), dma((2,))], smem=(0,), odd=1,
-        after=(x_token,),
-    )(weight, labels)
+    (nodes,) = call(columns_kernel, [(96, 128)], n_in=2, after=(x_token,))(displacement, labels)
+    near, far = call(weight_edges_kernel, [edge_x, edge_x], n_in=2, smem=(0,), odd=1, after=(nodes,))(weight, labels)
     w_near = swap_route(near, "gx", 0)
     w_far = swap_route(far, "gx", 1)
-    (nodes,) = call(columns_kernel, [(96, 128)], n_in=2, after=(near,))(displacement, labels)
     top, second = call(strain_kernel, [field3, field3], n_in=8, smem=(0, 1, 2))(
         weight, poisson, applied_strain, displacement, xm, ym, xym, labels
     )
@@ -559,12 +561,14 @@
     weights, near, far = call(
         weights_x_kernel, [field3, edge_y, edge_y], n_in=4, smem=(0,), odd=1, after=(mine,)
     )(weight, labels, w_near, w_far)
-    w_near, w_far = swap_route(near, "gy", 0), swap_route(far, "gy", 1)
+    w_near = swap_route(near, "gy", 0)
+    w_far = swap_route(far, "gy", 1)
     (local,) = call(z_local_kernel, [field3], n_in=2, after=(near,))(top, gz)
     top, near, far, second_last = call(
         top_z_kernel, [field3, edge_y, edge_y, (32, 128)], scratch=[vmem((32, 128), F32)], n_in=7, smem=(0, 1, 2), odd=3
     )(weight, poisson, applied_strain, local, mine, peer, gh)
-    t_near, t_far = swap_route(near, "gy", 0), swap_route(far, "gy", 1)
+    t_near = swap_route(near, "gy", 0)
+    t_far = swap_route(far, "gy", 1)
     phases = call(
         phases_kernel, [field3] * 5, n_in=8, smem=range(5), after=(near,)
     )(modulus, poisson, threshold, ductility, brittleness, labels, second, second_last)
@@ -573,9 +577,10 @@
     )(weights, w_near, w_far, gy, gz)
     z_token = cols
     cols = shift_route(cols, ("gz",), (1,))
-    top, near, far = call(
-        top_y_kernel, [field3, edge_x, edge_x], n_in=4, odd=0, after=(z_token,)
-    )(top, t_near, t_far, gy)
+    (far,) = call(top_y_far_kernel, [edge_x], n_in=4, odd=0, after=(z_token,))(top, t_near, t_far, gy)
+    top, near = call(top_y_kernel, [field3, edge_x], n_in=5, odd=0)(
+        top, t_near, t_far, gy, far
+    )
     (inverse,) = call(weights_z_kernel, [field3], n_in=3, after=(near,))(weights, cols, gh)
     far = swap_route(far, "gx", 1)
     near = swap_route(near, "gx", 0)

time: 67.3 us -> 71.1 us (1.056)
  the two profiles are of different devices: /device:TPU:32 before, /device:TPU:1 now
where the time goes in v2:
time: 71.1 us; the launch traced here: 71 us
  starting transfers between devices  28.1 us (40%)
  waiting for transfers between devices  20.1 us (28%)
  Pallas kernels  19.8 us (28%)
  local copies, waits for them, and re-layouts  2.06 us (3%)
  between operations  0.89 us (1%)
    pallas_call x15, Pallas kernels, call(): return lambda *args: built(*args, *after)  19.8 us
    ppermute x5, starting transfers between devices, shift_route(): return lax.ppermute(block, axes if len(axes) > 1 else axes[0], route)  17.2 us
    ppermute x5, waiting for transfers between devices, shift_route(): return lax.ppermute(block, axes if len(axes) > 1 else axes[0], route)  13 us
    ppermute x8, starting transfers between devices, swap_route(): return lax.ppermute(block, axis, route)  10.9 us
    ppermute x8, waiting for transfers between devices, swap_route(): return lax.ppermute(block, axis, route)  7.1 us
    unnamed x26, local copies, waits for them, and re-layouts  2.06 us
  transfers between devices with their start and end apart: 13, of which 4 were waited for; matrix products, arithmetic and copies ran while one was open for 0% of the time, Pallas kernels for 22%

profile of v2, /device:TPU:1, one launch (start us, length us, event | category | flops | bytes accessed | tf_op | source)
XLA Modules:
  0.0 71.0 jit_solution(4879470109716436980)
XLA Ops:
  0.6 0.0 copy-start
  0.6 0.0 copy-start.2
  0.6 2.0 %copy-done.2 = f32[3,32,32,256]{3,2,1,0:T(8,128)S(1)} copy-done((f32[3,32,32,256]{3,2,1,0:T(8,128)S(1)}, f32[3,32,32,256]{3,2,1,0:T(8,128)}, u32[]{:S(2)}) %copy-start.2) | copy-done | bytes 3145752
  2.6 0.3 shard_map.149
  2.9 0.0 copy-start.7
  2.9 0.0 copy-start.8
  2.9 0.0 copy-done
  2.9 1.2 %shard_map.151.refs_2_.refs_1_ = f32[96,128]{1,0:T(8,128)S(1)} custom-call(f32[3,32,32,256]{3,2,1,0:T(8,128)S(1)} %get-tuple-element.28.refs_3_.refs_0_, s32[32,32,256]{2,1,0:T(8,128)S(1)} %copy-done, f32[3,32,256]{2,1,0:T(8,128)S(1)} %get-tuple-element.29.refs_2_), custom_call_target="tpu_custom_call" | custom-call | tf_op jit(solution)/shard_map/pallas_call | solution.py:94
  4.2 0.0 copy-done.6
  4.2 0.7 shard_map.152
  4.8 3.3 %collective-permute-start.3 = (f32[8,32,256]{2,1,0:T(8,128)S(1)}, f32[8,32,256]{2,1,0:T(8,128)S(1)}, u32[]{:S(2)}, u32[]{:S(2)}) collective-permute-start(f32[8,32,256]{2,1,0:T(8,128)S(1)} %get-tuple-element.33), channel_id=1, source_target_pairs={{0,32},{32,0},{64,96},{96,64},{128,160},{160,128},{192,224},{224,1... | collective-permute-start | bytes 786440 | tf_op jit(solution)/shard_map/ppermute | solution.py:65
  8.1 0.0 collective-permute-start.4
  8.1 4.8 %collective-permute-start.1 = (f32[3,32,256]{2,1,0:T(8,128)S(1)}, f32[3,32,256]{2,1,0:T(8,128)S(1)}, u32[]{:S(2)}, u32[]{:S(2)}) collective-permute-start(f32[3,32,256]{2,1,0:T(8,128)S(1)} %get-tuple-element.30), channel_id=1, source_target_pairs={{0,30},{2,0},{4,2},{6,4},{8,6},{10,8},{12,10},{14,12},{16,14},{18,... | collective-permute-start | bytes 294920 | tf_op jit(solution)/shard_map/ppermute | solution.py:56
  13.0 3.4 %collective-permute-start = (f32[3,32,256]{2,1,0:T(8,128)S(1)}, f32[3,32,256]{2,1,0:T(8,128)S(1)}, u32[]{:S(2)}, u32[]{:S(2)}) collective-permute-start(f32[3,32,256]{2,1,0:T(8,128)S(1)} %get-tuple-element.29.refs_2_), channel_id=1, source_target_pairs={{0,224},{32,0},{64,32},{96,64},{128,96},{160,128},{192,160},{224,1... | collective-permute-start | bytes 294920 | tf_op jit(solution)/shard_map/ppermute | solution.py:56
  16.4 0.4 collective-permute-start.2
  16.7 3.6 %collective-permute-done.2.refs_6_.refs_4_ = f32[8,256]{1,0:T(8,128)S(1)} collective-permute-done((f32[8,256]{1,0:T(8,128)S(1)}, f32[8,256]{1,0:T(8,128)S(1)}, u32[]{:S(2)}, u32[]{:S(2)}) %collective-permute-start.2) | collective-permute-done | bytes 8224 | tf_op jit(solution)/shard_map/ppermute | solution.py:56
  20.3 0.0 collective-permute-done.1.refs_5_.refs_3_
  20.4 0.0 collective-permute-done.refs_4_.refs_2_
  20.4 0.0 copy-done.7
  20.4 0.0 copy-done.8
  20.4 5.3 %shard_map.150 = (f32[32,32,256]{2,1,0:T(8,128)S(1)}, f32[32,32,256]{2,1,0:T(8,128)S(1)}) custom-call(f32[4]{0:T(128)S(1)} %copy-done.6, f32[4]{0:T(128)S(1)} %copy-done.7, f32[6]{0:T(128)S(1)} %copy-done.8, f32[3,32,32,256]{3,2,1,0:T(8,128)S(1)} %get-tuple-element.28.refs_3_.refs_0_, f32[3,32,256]{2,1,0:T(8,128)S(1)} %collective-permute-done.refs_4_.refs_2_, ...), custom_call_target="tpu_custom_call" | custom-call | tf_op jit(solution)/shard_map/pallas_call | solution.py:94
  25.7 0.0 copy-start.5
  25.7 0.6 shard_map.153.refs_4_
  26.2 0.0 copy-start.9
  26.3 0.0 copy-start.10
  26.3 0.0 copy-start.11
  26.3 0.0 copy-start.12
  26.3 4.3 %collective-permute-start.5 = (f32[240,128]{1,0:T(8,128)S(1)}, f32[240,128]{1,0:T(8,128)S(1)}, u32[]{:S(2)}, u32[]{:S(2)}) collective-permute-start(f32[240,128]{1,0:T(8,128)S(1)} %shard_map.153.refs_4_), channel_id=1, source_target_pairs={{0,1},{1,0},{2,3},{3,2},{4,5},{5,4},{6,7},{7,6},{8,9},{9,8},{10,11... | collective-permute-start | bytes 368648 | tf_op jit(solution)/shard_map/ppermute | solution.py:56
  30.6 0.0 collective-permute-done.3.refs_2_
  30.6 0.0 collective-permute-done.4.refs_3_
  30.6 1.8 %shard_map.154 = (f32[32,32,256]{2,1,0:T(8,128)S(1)}, f32[32,8,256]{2,1,0:T(8,128)S(1)}, f32[32,8,256]{2,1,0:T(8,128)S(1)}) custom-call(f32[4]{0:T(128)S(1)} %copy-done.6, s32[32,32,256]{2,1,0:T(8,128)S(1)} %copy-done, f32[8,32,256]{2,1,0:T(8,128)S(1)} %collective-permute-done.3.refs_2_, f32[8,32,256]{2,1,0:T(8,128)S(1)} %collective-permute-done.4.refs_3_, ...), custom_call_target="tpu_custom_call" | custom-call | tf_op jit(solution)/shard_map/pallas_call | solution.py:94
  32.4 0.0 copy-start.4
  32.4 0.8 %collective-permute-start.8 = (f32[32,8,256]{2,1,0:T(8,128)S(1)}, f32[32,8,256]{2,1,0:T(8,128)S(1)}, u32[]{:S(2)}, u32[]{:S(2)}) collective-permute-start(f32[32,8,256]{2,1,0:T(8,128)S(1)} %get-tuple-element.35.refs_2_), channel_id=1, source_target_pairs={{0,2},{2,0},{4,6},{6,4},{8,10},{10,8},{12,14},{14,12},{16,18},{18,... | collective-permute-start | bytes 786440 | tf_op jit(solution)/shard_map/ppermute | solution.py:65
  33.3 0.0 copy-done.3
  33.3 0.6 shard_map.155.refs_3_
  33.9 3.9 %collective-permute-start.9 = (f32[32,8,256]{2,1,0:T(8,128)S(1)}, f32[32,8,256]{2,1,0:T(8,128)S(1)}, u32[]{:S(2)}, u32[]{:S(2)}) collective-permute-start(f32[32,8,256]{2,1,0:T(8,128)S(1)} %get-tuple-element.40), channel_id=1, source_target_pairs={{2,4},{4,2},{6,8},{8,6},{10,12},{12,10},{14,16},{16,14},{18,20},{2... | collective-permute-start | bytes 786440 | tf_op jit(solution)/shard_map/ppermute | solution.py:65
  37.7 0.0 collective-permute-done.5.refs_5_
  37.7 0.0 copy-done.5
  37.7 1.5 %shard_map.156 = (f32[32,32,256]{2,1,0:T(8,128)S(1)}, f32[32,8,256]{2,1,0:T(8,128)S(1)}, f32[32,8,256]{2,1,0:T(8,128)S(1)}, f32[32,128]{1,0:T(8,128)S(1)}) custom-call(f32[4]{0:T(128)S(1)} %copy-done.6, f32[4]{0:T(128)S(1)} %copy-done.7, f32[6]{0:T(128)S(1)} %copy-done.8, f32[32,32,256]{2,1,0:T(8,128)S(1)} %shard_map.155.refs_3_, ...), custom_call_target="tpu_custom_call" | custom-call | tf_op jit(solution)/shard_map/pallas_call | solution.py:94
  39.3 1.3 %collective-permute-start.7 = (f32[32,8,256]{2,1,0:T(8,128)S(1)}, f32[32,8,256]{2,1,0:T(8,128)S(1)}, u32[]{:S(2)}, u32[]{:S(2)}) collective-permute-start(f32[32,8,256]{2,1,0:T(8,128)S(1)} %get-tuple-element.38), channel_id=1, source_target_pairs={{2,4},{4,2},{6,8},{8,6},{10,12},{12,10},{14,16},{16,14},{18,20},{2... | collective-permute-start | bytes 786440 | tf_op jit(solution)/shard_map/ppermute | solution.py:65
  40.6 0.0 collective-permute-start.6
  40.6 0.0 copy-done.9
  40.6 0.0 copy-done.10
  40.6 0.0 copy-done.11
  40.6 0.0 copy-done.12
  40.6 1.5 %shard_map.157 = (f32[32,32,256]{2,1,0:T(8,128)S(1)}, f32[32,32,256]{2,1,0:T(8,128)S(1)}, f32[32,32,256]{2,1,0:T(8,128)S(1)}, f32[32,32,256]{2,1,0:T(8,128)S(1)}, f32[32,32,256]{2,1,0:T(8,128)S(1)}) custom-call(f32[4]{0:T(128)S(1)} %copy-done.9, f32[4]{0:T(128)S(1)} %copy-done.7, f32[4]{0:T(128)S(1)} %copy-done.10, f32[4]{0:T(128)S(1)} %copy-done.11, ...), custom_call_target="tpu_custom_call" | custom-call | tf_op jit(solution)/shard_map/pallas_call | solution.py:94
  42.1 3.0 %collective-permute-done.9.refs_2_ = f32[32,8,256]{2,1,0:T(8,128)S(1)} collective-permute-done((f32[32,8,256]{2,1,0:T(8,128)S(1)}, f32[32,8,256]{2,1,0:T(8,128)S(1)}, u32[]{:S(2)}, u32[]{:S(2)}) %collective-permute-start.9) | collective-permute-done | bytes 262176 | tf_op jit(solution)/shard_map/ppermute | solution.py:65
  45.2 0.0 collective-permute-done.8.refs_1_
  45.2 1.5 %shard_map.158 = (f32[32,32,256]{2,1,0:T(8,128)S(1)}, f32[128,128]{1,0:T(8,128)S(1)}) custom-call(f32[32,32,256]{2,1,0:T(8,128)S(1)} %get-tuple-element.39.refs_0_, f32[32,8,256]{2,1,0:T(8,128)S(1)} %collective-permute-done.8.refs_1_, f32[32,8,256]{2,1,0:T(8,128)S(1)} %collective-permute-done.9.refs_2_, bf16[32,144]{1,0:T(8,128)(2,1)S(1)} %copy-done.4, ...), custom_call_target="tpu_custom_call" | custom-call | tf_op jit(solution)/shard_map/pallas_call | solution.py:94
  46.7 0.0 copy-start.1
  46.7 4.1 %collective-permute-done.7.refs_2_ = f32[32,8,256]{2,1,0:T(8,128)S(1)} collective-permute-done((f32[32,8,256]{2,1,0:T(8,128)S(1)}, f32[32,8,256]{2,1,0:T(8,128)S(1)}, u32[]{:S(2)}, u32[]{:S(2)}) %collective-permute-start.7) | collective-permute-done | bytes 262176 | tf_op jit(solution)/shard_map/ppermute | solution.py:65
  50.7 0.0 collective-permute-done.6.refs_1_
  50.7 0.2 shard_map.159.refs_4_
  50.9 0.7 %shard_map.160 = (f32[32,32,256]{2,1,0:T(8,128)S(1)}, f32[8,32,256]{2,1,0:T(8,128)S(1)}) custom-call(f32[32,32,256]{2,1,0:T(8,128)S(1)} %get-tuple-element.36.refs_0_, f32[32,8,256]{2,1,0:T(8,128)S(1)} %collective-permute-done.6.refs_1_, f32[32,8,256]{2,1,0:T(8,128)S(1)} %collective-permute-done.7.refs_2_, bf16[32,144]{1,0:T(8,128)(2,1)S(1)} %copy-done.4, ...), custom_call_target="tpu_custom_call" | custom-call | tf_op jit(solution)/shard_map/pallas_call | solution.py:94
  51.7 1.0 %collective-permute-start.12 = (f32[8,32,256]{2,1,0:T(8,128)S(1)}, f32[8,32,256]{2,1,0:T(8,128)S(1)}, u32[]{:S(2)}, u32[]{:S(2)}) collective-permute-start(f32[8,32,256]{2,1,0:T(8,128)S(1)} %get-tuple-element.47.refs_3_), channel_id=1, source_target_pairs={{0,32},{32,0},{64,96},{96,64},{128,160},{160,128},{192,224},{224,1... | collective-permute-start | bytes 786440 | tf_op jit(solution)/shard_map/ppermute | solution.py:65
  52.6 0.6 collective-permute-start.10
  53.2 4.3 %collective-permute-start.11 = (f32[128,128]{1,0:T(8,128)S(1)}, f32[128,128]{1,0:T(8,128)S(1)}, u32[]{:S(2)}, u32[]{:S(2)}) collective-permute-start(f32[128,128]{1,0:T(8,128)S(1)} %get-tuple-element.44.refs_4_), channel_id=1, source_target_pairs={{0,1},{1,0},{2,3},{3,2},{4,5},{5,4},{6,7},{7,6},{8,9},{9,8},{10,11... | collective-permute-start | bytes 196616 | tf_op jit(solution)/shard_map/ppermute | solution.py:56
  57.6 9.4 %collective-permute-done.11.refs_1_ = f32[128,128]{1,0:T(8,128)S(1)} collective-permute-done((f32[128,128]{1,0:T(8,128)S(1)}, f32[128,128]{1,0:T(8,128)S(1)}, u32[]{:S(2)}, u32[]{:S(2)}) %collective-permute-start.11) | collective-permute-done | bytes 65568 | tf_op jit(solution)/shard_map/ppermute | solution.py:56
  66.9 0.6 shard_map.161.refs_2_
  67.5 0.0 collective-permute-done.12.refs_1_
  67.5 0.0 copy-done.1
  67.6 2.1 %shard_map.162 = (f32[32,32,256]{2,1,0:T(8,128)}, f32[32,32,256]{2,1,0:T(8,128)}) custom-call(f32[32,32,256]{2,1,0:T(8,128)S(1)} %get-tuple-element.45.refs_0_, f32[8,32,256]{2,1,0:T(8,128)S(1)} %collective-permute-done.12.refs_1_, f32[32,32,256]{2,1,0:T(8,128)S(1)} %shard_map.161.refs_2_, f32[32,32,256]{2,1,0:T(8,128)S(1)} %copy-done.1, ...), custom_call_target="tpu_custom_call" | custom-call | tf_op jit(solution)/shard_map/pallas_call | solution.py:94
  69.6 0.0 collective-permute-done.10.refs_1_
  69.6 1.3 %shard_map.163 = (f32[32,32,256]{2,1,0:T(8,128)}, f32[32,32,256]{2,1,0:T(8,128)}) custom-call(f32[32,32,256]{2,1,0:T(8,128)S(1)} %get-tuple-element.45.refs_0_, f32[8,32,256]{2,1,0:T(8,128)S(1)} %collective-permute-done.10.refs_1_, f32[32,32,256]{2,1,0:T(8,128)S(1)} %shard_map.161.refs_2_, ...), custom_call_target="tpu_custom_call", output_to_operand_aliasing={{0}: (9, {}), {1}: (10, {})} | custom-call | tf_op jit(solution)/shard_map/pallas_call | solution.py:94
  (3 shorter events, 0.0 us)
Async XLA Ops:
  0.6 2.3 %copy-start = (s32[32,32,256]{2,1,0:T(8,128)S(1)}, s32[32,32,256]{2,1,0:T(8,128)}, u32[]{:S(2)}) copy-start(s32[32,32,256]{2,1,0:T(8,128)} %refs_5_.1) | copy-start | bytes 3145732
  0.6 2.0 %copy-start.2 = (f32[3,32,32,256]{3,2,1,0:T(8,128)S(1)}, f32[3,32,32,256]{3,2,1,0:T(8,128)}, u32[]{:S(2)}) copy-start(f32[3,32,32,256]{3,2,1,0:T(8,128)} %refs_0_.6) | copy-start | bytes 9437188
  2.6 1.5 %copy-start.6 = (f32[4]{0:T(128)S(1)}, f32[4]{0:T(128)}, u32[]{:S(2)}) copy-start(f32[4]{0:T(128)} %refs_0_.10) | copy-start | bytes 52
  2.9 17.5 %copy-start.7 = (f32[4]{0:T(128)S(1)}, f32[4]{0:T(128)}, u32[]{:S(2)}) copy-start(f32[4]{0:T(128)} %refs_1_.11) | copy-start | bytes 52
  2.9 17.4 %copy-start.8 = (f32[6]{0:T(128)S(1)}, f32[6]{0:T(128)}, u32[]{:S(2)}) copy-start(f32[6]{0:T(128)} %refs_2_.5) | copy-start | bytes 76
  4.8 25.8 %collective-permute-start.3 = (f32[8,32,256]{2,1,0:T(8,128)S(1)}, f32[8,32,256]{2,1,0:T(8,128)S(1)}, u32[]{:S(2)}, u32[]{:S(2)}) collective-permute-start(f32[8,32,256]{2,1,0:T(8,128)S(1)} %get-tuple-element.33), channel_id=1, source_target_pairs={{0,32},{32,0},{64,96},{96,64},{128,160},{160,128},{192,224},{224,1... | collective-permute-start | bytes 786440 | tf_op jit(solution)/shard_map/ppermute | solution.py:65
  8.1 22.5 %collective-permute-start.4 = (f32[8,32,256]{2,1,0:T(8,128)S(1)}, f32[8,32,256]{2,1,0:T(8,128)S(1)}, u32[]{:S(2)}, u32[]{:S(2)}) collective-permute-start(f32[8,32,256]{2,1,0:T(8,128)S(1)} %get-tuple-element.34), channel_id=1, source_target_pairs={{32,64},{64,32},{96,128},{128,96},{160,192},{192,160},{224,0},{0,2... | collective-permute-start | bytes 786440 | tf_op jit(solution)/shard_map/ppermute | solution.py:65
  8.1 12.2 %collective-permute-start.1 = (f32[3,32,256]{2,1,0:T(8,128)S(1)}, f32[3,32,256]{2,1,0:T(8,128)S(1)}, u32[]{:S(2)}, u32[]{:S(2)}) collective-permute-start(f32[3,32,256]{2,1,0:T(8,128)S(1)} %get-tuple-element.30), channel_id=1, source_target_pairs={{0,30},{2,0},{4,2},{6,4},{8,6},{10,8},{12,10},{14,12},{16,14},{18,... | collective-permute-start | bytes 294920 | tf_op jit(solution)/shard_map/ppermute | solution.py:56
  13.0 7.4 %collective-permute-start = (f32[3,32,256]{2,1,0:T(8,128)S(1)}, f32[3,32,256]{2,1,0:T(8,128)S(1)}, u32[]{:S(2)}, u32[]{:S(2)}) collective-permute-start(f32[3,32,256]{2,1,0:T(8,128)S(1)} %get-tuple-element.29.refs_2_), channel_id=1, source_target_pairs={{0,224},{32,0},{64,32},{96,64},{128,96},{160,128},{192,160},{224,1... | collective-permute-start | bytes 294920 | tf_op jit(solution)/shard_map/ppermute | solution.py:56
  16.4 16.9 %copy-start.3 = (bf16[2,256,256]{2,1,0:T(8,128)(2,1)S(1)}, bf16[2,256,256]{2,1,0:T(8,128)(2,1)}, u32[]{:S(2)}) copy-start(bf16[2,256,256]{2,1,0:T(8,128)(2,1)} %constant.14.refs_1_.refs_4_) | copy-start | bytes 786436
  16.4 4.0 %collective-permute-start.2 = (f32[8,256]{1,0:T(8,128)S(1)}, f32[8,256]{1,0:T(8,128)S(1)}, u32[]{:S(2)}, u32[]{:S(2)}) collective-permute-start(f32[8,256]{1,0:T(8,128)S(1)} %get-tuple-element.31), channel_id=1, source_target_pairs={{0,254},{2,224},{4,226},{6,228},{8,230},{10,232},{12,234},{14,236}... | collective-permute-start | bytes 24584 | tf_op jit(solution)/shard_map/ppermute | solution.py:56
  25.7 12.1 %copy-start.5 = (bf16[72,256]{1,0:T(8,128)(2,1)S(1)}, bf16[72,256]{1,0:T(8,128)(2,1)}, u32[]{:S(2)}) copy-start(bf16[72,256]{1,0:T(8,128)(2,1)} %constant.10.clone.refs_6_.refs_2_) | copy-start | bytes 110596
  26.2 14.4 %copy-start.9 = (f32[4]{0:T(128)S(1)}, f32[4]{0:T(128)}, u32[]{:S(2)}) copy-start(f32[4]{0:T(128)} %refs_0_.11) | copy-start | bytes 52
  26.3 14.3 %copy-start.10 = (f32[4]{0:T(128)S(1)}, f32[4]{0:T(128)}, u32[]{:S(2)}) copy-start(f32[4]{0:T(128)} %refs_2_.6) | copy-start | bytes 52
  26.3 14.3 %copy-start.11 = (f32[4]{0:T(128)S(1)}, f32[4]{0:T(128)}, u32[]{:S(2)}) copy-start(f32[4]{0:T(128)} %refs_3_.6) | copy-start | bytes 52
  26.3 14.3 %copy-start.12 = (f32[4]{0:T(128)S(1)}, f32[4]{0:T(128)}, u32[]{:S(2)}) copy-start(f32[4]{0:T(128)} %refs_4_.1) | copy-start | bytes 52
  26.3 11.4 %collective-permute-start.5 = (f32[240,128]{1,0:T(8,128)S(1)}, f32[240,128]{1,0:T(8,128)S(1)}, u32[]{:S(2)}, u32[]{:S(2)}) collective-permute-start(f32[240,128]{1,0:T(8,128)S(1)} %shard_map.153.refs_4_), channel_id=1, source_target_pairs={{0,1},{1,0},{2,3},{3,2},{4,5},{5,4},{6,7},{7,6},{8,9},{9,8},{10,11... | collective-permute-start | bytes 368648 | tf_op jit(solution)/shard_map/ppermute | solution.py:56
  32.4 12.7 %copy-start.4 = (bf16[32,144]{1,0:T(8,128)(2,1)S(1)}, bf16[32,144]{1,0:T(8,128)(2,1)}, u32[]{:S(2)}) copy-start(bf16[32,144]{1,0:T(8,128)(2,1)} %constant.11.clone.refs_3_) | copy-start | bytes 27652
  32.4 12.7 %collective-permute-start.8 = (f32[32,8,256]{2,1,0:T(8,128)S(1)}, f32[32,8,256]{2,1,0:T(8,128)S(1)}, u32[]{:S(2)}, u32[]{:S(2)}) collective-permute-start(f32[32,8,256]{2,1,0:T(8,128)S(1)} %get-tuple-element.35.refs_2_), channel_id=1, source_target_pairs={{0,2},{2,0},{4,6},{6,4},{8,10},{10,8},{12,14},{14,12},{16,18},{18,... | collective-permute-start | bytes 786440 | tf_op jit(solution)/shard_map/ppermute | solution.py:65
  33.9 11.3 %collective-permute-start.9 = (f32[32,8,256]{2,1,0:T(8,128)S(1)}, f32[32,8,256]{2,1,0:T(8,128)S(1)}, u32[]{:S(2)}, u32[]{:S(2)}) collective-permute-start(f32[32,8,256]{2,1,0:T(8,128)S(1)} %get-tuple-element.40), channel_id=1, source_target_pairs={{2,4},{4,2},{6,8},{8,6},{10,12},{12,10},{14,16},{16,14},{18,20},{2... | collective-permute-start | bytes 786440 | tf_op jit(solution)/shard_map/ppermute | solution.py:65
  39.3 11.5 %collective-permute-start.7 = (f32[32,8,256]{2,1,0:T(8,128)S(1)}, f32[32,8,256]{2,1,0:T(8,128)S(1)}, u32[]{:S(2)}, u32[]{:S(2)}) collective-permute-start(f32[32,8,256]{2,1,0:T(8,128)S(1)} %get-tuple-element.38), channel_id=1, source_target_pairs={{2,4},{4,2},{6,8},{8,6},{10,12},{12,10},{14,16},{16,14},{18,20},{2... | collective-permute-start | bytes 786440 | tf_op jit(solution)/shard_map/ppermute | solution.py:65
  40.6 10.1 %collective-permute-start.6 = (f32[32,8,256]{2,1,0:T(8,128)S(1)}, f32[32,8,256]{2,1,0:T(8,128)S(1)}, u32[]{:S(2)}, u32[]{:S(2)}) collective-permute-start(f32[32,8,256]{2,1,0:T(8,128)S(1)} %get-tuple-element.37.refs_8_), channel_id=1, source_target_pairs={{0,2},{2,0},{4,6},{6,4},{8,10},{10,8},{12,14},{14,12},{16,18},{18,... | collective-permute-start | bytes 786440 | tf_op jit(solution)/shard_map/ppermute | solution.py:65
  46.7 20.9 %copy-start.1 = (f32[32,32,256]{2,1,0:T(8,128)S(1)}, f32[32,32,256]{2,1,0:T(8,128)}, u32[]{:S(2)}) copy-start(f32[32,32,256]{2,1,0:T(8,128)} %refs_3_.8) | copy-start | bytes 3145732
  51.7 15.9 %collective-permute-start.12 = (f32[8,32,256]{2,1,0:T(8,128)S(1)}, f32[8,32,256]{2,1,0:T(8,128)S(1)}, u32[]{:S(2)}, u32[]{:S(2)}) collective-permute-start(f32[8,32,256]{2,1,0:T(8,128)S(1)} %get-tuple-element.47.refs_3_), channel_id=1, source_target_pairs={{0,32},{32,0},{64,96},{96,64},{128,160},{160,128},{192,224},{224,1... | collective-permute-start | bytes 786440 | tf_op jit(solution)/shard_map/ppermute | solution.py:65
  52.6 17.0 %collective-permute-start.10 = (f32[8,32,256]{2,1,0:T(8,128)S(1)}, f32[8,32,256]{2,1,0:T(8,128)S(1)}, u32[]{:S(2)}, u32[]{:S(2)}) collective-permute-start(f32[8,32,256]{2,1,0:T(8,128)S(1)} %shard_map.159.refs_4_), channel_id=1, source_target_pairs={{32,64},{64,32},{96,128},{128,96},{160,192},{192,160},{224,0},{0,2... | collective-permute-start | bytes 786440 | tf_op jit(solution)/shard_map/ppermute | solution.py:65
  53.2 13.7 %collective-permute-start.11 = (f32[128,128]{1,0:T(8,128)S(1)}, f32[128,128]{1,0:T(8,128)S(1)}, u32[]{:S(2)}, u32[]{:S(2)}) collective-permute-start(f32[128,128]{1,0:T(8,128)S(1)} %get-tuple-element.44.refs_4_), channel_id=1, source_target_pairs={{0,1},{1,0},{2,3},{3,2},{4,5},{5,4},{6,7},{7,6},{8,9},{9,8},{10,11... | collective-permute-start | bytes 196616 | tf_op jit(solution)/shard_map/ppermute | solution.py:56
